TPU v7x, 32 devices: a whole 2x2x4 slice. The times are simulated.
32 devices in a mesh: groups: 1, row: 16 (over z, y, x), col: 2 (over core).
Axes of the slice: x: 2, y: 2, z: 4, core: 2. Of those that a mesh axis runs over, the one named last changes fastest.
Arguments:
- image: bfloat16 [64, 64, 1408], P(('groups', 'row'), None, 'col'), may hold values from -6 to 6
- kernel: float32 [7, 7, 1408], P(None, None, 'col'), may hold values from -0.875 to 0.875
- ln_gain: float32 [1408], replicated, may hold values from 0.1 to 1.9
- ln_bias: float32 [1408], replicated, may hold values from -3 to 3
- layer_scale: float32 [1408], replicated, may hold values from 0.3 to 1.5
- w_in: bfloat16 [1408, 2816], P('row', 'col'), may hold values from -0.15625 to 0.15625
- w_out: bfloat16 [2816, 1408], P('col', 'row'), may hold values from -0.109375 to 0.109375
- cotangent: bfloat16 [64, 64, 1408], P(('groups', 'row'), None, 'col'), may hold values from -16 to 16
Outputs:
- result: bfloat16 [64, 64, 1408], P(('groups', 'row'), None, 'col')
- grad_image: bfloat16 [64, 64, 1408], P(('groups', 'row'), None, 'col')
- grad_kernel: float32 [7, 7, 1408], P('groups', None, 'col')
- grad_params: float32 [3, 1408], P('groups', 'col')
All inputs are finite; a program needn't handle non-finite values.
Results may differ from a plain program's by a relative error of at most 0.0057.
Values may be sent and summed in bfloat16 or wider, within the bound.
No kernel may reach another device: no remote copies, remote signals or barrier semaphores. Data moves between devices by JAX's collectives and lax.ppermute only.
A program may use at most 64 MiB of HBM per device.

v0:
```python
import functools
import math

import jax
import jax.numpy as jnp
from jax import lax
from jax.experimental import pallas as pl
from jax.experimental.pallas import tpu as pltpu
from jax.sharding import PartitionSpec as P

epsilon = 1e-06
VMEM = pl.BlockSpec(memory_space=pltpu.VMEM)
SMEM = pl.BlockSpec(memory_space=pltpu.SMEM)


def sent(value, axis, pairs):
    if value.ndim == 2 and value.shape[1] == 704:
        return lax.ppermute(value.reshape(4, -1, 704), axis, pairs).reshape(value.shape)
    return lax.ppermute(value, axis, pairs)


def exchanged(value, mask):
    count = lax.axis_size("row")
    return sent(value, "row", [(i, i ^ mask) for i in range(count)])


def siblings(value):
    return sent(value, "col", [(0, 1), (1, 0)])


def both(value):
    rows, width = value.shape
    pair = lax.all_gather(value.reshape(4, rows // 4, width), "col", axis=0, tiled=False)
    return pair.reshape(2, rows, width)


def after(value, *others):
    return lax.optimization_barrier((value, *others))[0]


def edges(even, low_rows, high_rows):
    return jnp.where(even, high_rows, low_rows), jnp.where(even, low_rows, high_rows)


def neighbours(direct, handed):
    count = lax.axis_size("row")
    through = exchanged(handed, 1)
    pairs = [(i, i + 2) for i in range(0, count - 2, 2)] + [(i, i - 2) for i in range(3, count, 2)]
    return exchanged(direct, 1), lax.ppermute(through, "row", pairs)


def call(body, outs, operands, name, scalars=(), scratch=(), flops=0, limit=24):
    moved = sum(math.prod(o.shape) * o.dtype.itemsize for o in list(outs) + list(operands))
    return pl.pallas_call(
        body,
        out_shape=tuple(outs),
        in_specs=[SMEM] * len(scalars) + [VMEM] * len(operands),
        out_specs=(VMEM,) * len(outs),
        scratch_shapes=list(scratch),
        compiler_params=pltpu.CompilerParams(vmem_limit_bytes=limit << 20),
        cost_estimate=pl.CostEstimate(flops=flops, bytes_accessed=moved, transcendentals=0),
        name=name,
    )(*scalars, *operands)


def spans(extent, step):
    return [(at, min(step, extent - at)) for at in range(0, extent, step)]


def f32(*shape):
    return jax.ShapeDtypeStruct(shape, jnp.float32)


def bf16(*shape):
    return jax.ShapeDtypeStruct(shape, jnp.bfloat16)


def each_lanes(width, body):
    full = width // 128

    def step(index, carry):
        body(pl.ds(pl.multiple_of(index * 128, 128), 128))
        return carry

    lax.fori_loop(0, full, step, 0)
    if width % 128:
        body(pl.ds(full * 128, width % 128))


def fill(rows_all, place, near, middle, beyond):
    rows = middle.shape[0]
    even = jnp.bitwise_and(place[0], 1) == 0
    rows_all[3 : 3 + rows] = middle[...].astype(jnp.float32)

    @pl.when(even)
    def _():
        rows_all[0:3] = beyond[...].astype(jnp.float32)
        rows_all[3 + rows :] = near[...].astype(jnp.float32)

    @pl.when(jnp.logical_not(even))
    def _():
        rows_all[0:3] = near[...].astype(jnp.float32)
        rows_all[3 + rows :] = beyond[...].astype(jnp.float32)


def clear_borders(ref, breadth):
    edge = ref.shape[:-2] + (8, ref.shape[-1])
    ref[..., 0:8, :] = jnp.zeros(edge, jnp.float32)
    ref[..., 8 + breadth :, :] = jnp.zeros(edge, jnp.float32)


def filtered(rows_all, kernel, shifted, rows, breadth, lanes, flip):
    size = lanes.size
    for col in range(7):
        total = [None] * rows
        for row in range(rows + 6):
            block = rows_all[row, :, lanes]
            for tap in range(7):
                at = row - tap
                if 0 <= at < rows:
                    a, b = (6 - tap, 6 - col) if flip else (tap, col)
                    term = kernel[a, b : b + 1, lanes] * block
                    total[at] = term if total[at] is None else total[at] + term
        for at in range(rows):
            shifted[col, at, 8 : 8 + breadth, 0:size] = total[at]
    results = []
    for at in range(rows):
        value = shifted[0, at, 5 : 5 + breadth, 0:size]
        for col in range(1, 7):
            value = value + shifted[col, at, 5 + col : 5 + col + breadth, 0:size]
        results.append(value)
    return results


def conv_body(place, near, middle, beyond, kernel, conved, stats, rows_all, shifted):
    rows, breadth, width = middle.shape
    fill(rows_all, place, near, middle, beyond)
    clear_borders(shifted, breadth)

    def part(lanes):
        for row, value in enumerate(filtered(rows_all, kernel, shifted, rows, breadth, lanes, False)):
            conved[row * breadth : (row + 1) * breadth, lanes] = value

    each_lanes(width, part)
    values = conved[...]
    mean = jnp.sum(values, axis=1, keepdims=True) * (1.0 / width)
    centred = values - mean
    stats[:, 0:1] = mean
    stats[:, 1:2] = jnp.sum(centred * centred, axis=1, keepdims=True)


def norm_body(conved, mine, other, params, normal, inverse, normed):
    width = conved.shape[1]
    average = 0.5 * (mine[:, 0:1] + other[:, 0:1])
    apart = mine[:, 0:1] - other[:, 0:1]
    variance = (mine[:, 1:2] + other[:, 1:2]) * (0.5 / width) + 0.25 * apart * apart
    inv_std = lax.rsqrt(variance + epsilon)
    value = (conved[...] - average) * inv_std
    normal[...] = value
    inverse[...] = inv_std
    normed[...] = (value * params[0:1, :] + params[1:2, :]).astype(jnp.bfloat16)


def split_of(width):
    main = width // 2 // 128 * 128
    return main, width // 2 - main


def packed(w_in, w_out, which):
    main, tail = split_of(w_in.shape[1])
    mains = slice(which * main, (which + 1) * main)
    tails = slice(2 * main + which * tail, 2 * main + (which + 1) * tail)
    return jnp.concatenate(
        [w_in[:, mains], w_out[:, mains], w_in[:, tails], w_out[:, tails]], axis=1
    )


def mlp_body(place, n_own, n_far, s_own, s_far, *refs):
    blocks, outs, (whole, act, grad) = refs[:16], refs[16:20], refs[20:]
    rows, width = blocks[0].shape
    _, tokens, half = n_own.shape
    core = place[1]
    main, tail = split_of(width)
    for index, block in enumerate(blocks):
        mask = 2 * (index % 8) + index // 8
        source = jnp.bitwise_xor(place[0], mask)
        side = jnp.bitwise_xor(jnp.right_shift(source, 3), place[1])
        start = side * half + jnp.bitwise_and(source, 7) * rows
        whole[pl.ds(pl.multiple_of(start, 8), rows), :] = block[...]
    lower = lax.broadcasted_iota(jnp.int32, (tokens, 128), 1) < tail

    def product(pair, parts):
        def side(left, start):
            weights = jnp.concatenate(
                [whole[start : start + half, at : at + size] for at, size in parts], axis=1
            )
            return jnp.dot(left, weights, preferred_element_type=jnp.float32)

        return side(pair[core], 0) + side(pair[1 - core], half)

    last = (2 * main, 128)
    pieces = spans(main, 256)
    for group, (n_pair, s_pair) in enumerate(((n_own, s_own), (n_far, s_far))):
        where = slice(group * tokens, (group + 1) * tokens)
        for at, size in pieces:
            final = at + size == main
            hidden = product(n_pair, [(at, size)] + ([last] if final else []))
            slopes = product(s_pair, [(main + at, size)] + ([last] if final else []))
            if final:
                moved = pltpu.roll(slopes[:, size:], tail, 1)
                slopes = jnp.concatenate([slopes[:, :size], moved], axis=1)
            cumulative = 0.5 * (1.0 + lax.erf(hidden * (1.0 / math.sqrt(2.0))))
            slope = cumulative + hidden * jnp.exp(-0.5 * hidden * hidden) * (
                1.0 / math.sqrt(2.0 * math.pi)
            )
            value = hidden * cumulative
            back = slopes * slope
            if final:
                upper = pltpu.roll(jnp.where(lower, value[:, size:], 0.0), tail, 1)
                value = jnp.concatenate([value[:, :size], upper], axis=1)
                back = jnp.concatenate(
                    [back[:, :size], jnp.where(lower, back[:, size:], 0.0)], axis=1
                )
            act[where, at : at + value.shape[1]] = value.astype(jnp.bfloat16)
            grad[where, at : at + value.shape[1]] = back.astype(jnp.bfloat16)
    back_products(grad, whole, 0, outs)


def back_products(left, whole, first, outs):
    half = whole.shape[0] // 2
    tokens = left.shape[0] // 2
    main, _ = split_of(whole.shape[1])
    number = 0
    for side in (1, 0):
        for group in (1, 0):
            out = outs[number]
            number += 1
            for at, size in spans(half, 256):
                chosen = slice(side * half + at, side * half + at + size)
                weights = jnp.concatenate(
                    [whole[chosen, first : first + main], whole[chosen, 2 * main :]], axis=1
                )
                out[:, at : at + size] = lax.dot_general(
                    left[group * tokens : (group + 1) * tokens, :],
                    weights,
                    (((1,), (1,)), ((), ())),
                    preferred_element_type=jnp.float32,
                )


def branch_body(act, whole, *outs):
    main, _ = split_of(whole.shape[1])
    back_products(act, whole, main, outs)


def mlp(place, normed, scaled, blocks):
    _, tokens, half = normed[0].shape
    rows, width = blocks[0].shape
    main, tail = split_of(width)
    parts = (f32(tokens, half),) * 4
    *grads, whole, act = call(
        mlp_body,
        (*parts, bf16(2 * half, width), bf16(2 * tokens, main + 128)),
        (*normed, *scaled, *blocks),
        "mlp",
        scalars=(place,),
        scratch=[pltpu.VMEM((2 * tokens, main + 128), jnp.bfloat16)],
        flops=6 * tokens * half * 2 * width,
        limit=32,
    )
    acts = call(branch_body, parts, (act, whole), "branch", flops=2 * tokens * half * 2 * width)
    return *grads, *acts


def joined_body(mine, other, out):
    out[...] = (mine[...] + other[...]).astype(jnp.bfloat16)


def joined(mine, other):
    return call(joined_body, (bf16(*mine.shape),), (mine, other), "joined", flops=mine.size)[0]


def grad_body(mine, other, across, normal, params, norm_grad, stats):
    value = mine[...] + other[...] + across[...].astype(jnp.float32)
    norm_grad[...] = value
    hat = value * params[0:1, :]
    stats[:, 0:1] = jnp.sum(hat, axis=1, keepdims=True)
    stats[:, 1:2] = jnp.sum(hat * normal[...], axis=1, keepdims=True)


def field_body(place, norm_grad, mine, other, normal, inverse, params, field, direct, handed):
    rows, breadth, width = field.shape
    first = (mine[:, 0:1] + other[:, 0:1]) * (0.5 / width)
    second = (mine[:, 1:2] + other[:, 1:2]) * (0.5 / width)
    value = inverse[...] * (norm_grad[...] * params[0:1, :] - first - normal[...] * second)
    value = value.reshape(rows, breadth, width)
    field[...] = value
    narrow = value.astype(jnp.bfloat16)
    even = jnp.bitwise_and(place[0], 1) == 0

    @pl.when(even)
    def _():
        direct[...] = narrow[rows - 3 :]
        handed[...] = narrow[:3]

    @pl.when(jnp.logical_not(even))
    def _():
        direct[...] = narrow[:3]
        handed[...] = narrow[rows - 3 :]


def result_body(place, image, mine, other, across, cot, params, *refs):
    branch = mine[...] + other[...] + across[...].astype(jnp.float32)
    result = refs[4]
    result[...] = (image[...].astype(jnp.float32) + params[2:3, :] * branch).astype(jnp.bfloat16)
    last = jnp.sum(cot[...].astype(jnp.float32) * branch, axis=0, keepdims=True)
    mine_is = jnp.bitwise_and(place[0], 3)
    for mask in range(4):
        chunk, out = refs[mask], refs[5 + mask]
        out[...] = chunk[...]

        @pl.when(jnp.bitwise_xor(mine_is, mask) == 1)
        def _():
            out[0, 7:8, :] = last


def terms_body(
    place, field, near, middle, beyond, norm_grad, normal, c0, c1, c2, c3, rows_all, moved, sums
):
    rows, breadth, width = middle.shape
    fill(rows_all, place, near, middle, beyond)
    clear_borders(moved, breadth)
    sums[...] = jnp.zeros_like(sums)

    def part(lanes):
        moved[:, 8 : 8 + breadth, 0 : lanes.size] = field[:, :, lanes]
        for col in range(7):
            total = [None] * 7
            for at in range(rows):
                values = moved[at, 11 - col : 11 - col + breadth, 0 : lanes.size]
                for tap in range(7):
                    term = values * rows_all[at + tap, :, lanes]
                    term = jnp.sum(term.reshape(breadth // 8, 8, term.shape[1]), axis=0)
                    total[tap] = term if total[tap] is None else total[tap] + term
            for tap in range(7):
                sums[tap, col : col + 1, lanes] = jnp.sum(total[tap], axis=0, keepdims=True)

    each_lanes(width, part)
    sums[0, 7:8, :] = jnp.sum(norm_grad[...] * normal[...], axis=0, keepdims=True)
    sums[1, 7:8, :] = jnp.sum(norm_grad[...], axis=0, keepdims=True)
    for mask, chunk in enumerate((c0, c1, c2, c3)):
        chunk[...] = sums[pl.ds(2 * jnp.bitwise_xor(jnp.bitwise_and(place[0], 3), mask), 2)]


def back_body(place, near, middle, beyond, kernel, cot, out, rows_all, shifted):
    rows, breadth, width = middle.shape
    fill(rows_all, place, near, middle, beyond)
    clear_borders(shifted, breadth)

    def part(lanes):
        for row, value in enumerate(filtered(rows_all, kernel, shifted, rows, breadth, lanes, True)):
            out[row, :, lanes] = (cot[row, :, lanes].astype(jnp.float32) + value).astype(
                jnp.bfloat16
            )

    each_lanes(width, part)


def final_body(factor, place, c0, c1, c2, c3, kernel_sum, param_sum, sums):
    for mask, chunk in enumerate((c0, c1, c2, c3)):
        index = 2 * jnp.bitwise_xor(jnp.bitwise_and(place[0], 3), mask)
        sums[pl.ds(index, 2)] = chunk[...] * factor
    kernel_sum[...] = sums[0:7, 0:7, :]
    for row in range(3):
        param_sum[row : row + 1, :] = sums[row, 7:8, :]


def paired(image, kernel, ln_gain, ln_bias, layer_scale, w_in, w_out, cotangent):
    slab_rows, grid_cols, width_part = image.shape
    tokens = slab_rows * grid_cols
    row = lax.axis_index("row").astype(jnp.int32)
    column = lax.axis_index("col").astype(jnp.int32)
    place = jnp.stack([row, column])
    even = (row & 1) == 0
    direct, handed = edges(even, image[:3], image[slab_rows - 3 :])
    next_rows, beyond_rows = neighbours(direct, handed)

    w_in = after(w_in, direct, handed)
    first, second = packed(w_in, w_out.T, 0), packed(w_in, w_out.T, 1)
    near = {0: jnp.where(even, first, second)}
    far = {0: exchanged(jnp.where(even, second, first), 1)}
    near[8] = exchanged(near[0], 8)
    near[2] = exchanged(near[0], 2)
    near[4] = exchanged(after(near[0], near[2]), 4)
    shape = pltpu.VMEM((slab_rows + 6, grid_cols, width_part), jnp.float32)
    wide = pltpu.VMEM((7, slab_rows, grid_cols + 16, 128), jnp.float32)
    macs = 98 * tokens * width_part
    conved, stats = call(
        conv_body,
        (f32(tokens, width_part), f32(tokens, 2)),
        (next_rows, image, after(beyond_rows, far[0], near[2]), kernel),
        "conv",
        scalars=(place,),
        scratch=[shape, wide],
        flops=macs * 1000,
    )
    far[2] = exchanged(after(far[0], near[2]), 2)
    far[8] = exchanged(after(far[0], near[8]), 8)
    near[10] = exchanged(after(near[8], next_rows), 2)
    near[6] = exchanged(after(near[4], far[2]), 2)
    near[12] = exchanged(after(near[8], near[4]), 4)
    far[10] = exchanged(after(far[8], near[6]), 2)
    far[12] = exchanged(far[8], 4)
    near[14] = exchanged(after(near[12], near[10]), 2)
    far[4] = exchanged(after(far[0], near[12]), 4)
    far[14] = exchanged(after(far[12], far[10]), 2)
    far[6] = exchanged(after(far[2], far[12]), 4)
    weights = [near[m] for m in range(0, 16, 2)] + [far[m] for m in range(0, 16, 2)]

    params = jnp.stack([ln_gain, ln_bias, layer_scale]).reshape(3, 2, width_part)
    params = lax.dynamic_index_in_dim(params, column, 1, False)
    flat_cot = cotangent.reshape(tokens, width_part)
    scaled = (flat_cot.astype(jnp.float32) * params[2]).astype(jnp.bfloat16)
    scaled_far = exchanged(after(scaled, next_rows), 1)
    scaled_all = (both(scaled), both(scaled_far))

    normal, inverse, normed = call(
        norm_body,
        (f32(tokens, width_part), f32(tokens, 1), bf16(tokens, width_part)),
        (conved, stats, siblings(stats), params),
        "norm",
        flops=6 * tokens * width_part,
    )
    normed_far = exchanged(after(normed, scaled_far), 1)
    normed_all = (both(normed), both(normed_far))

    outs = mlp(place, normed_all, scaled_all, weights)
    grad_there_far, grad_there, grad_far, grad_own = outs[:4]
    act_there_far, act_there, act_far, act_own = outs[4:]
    grad_across = exchanged(joined(grad_far, siblings(grad_there_far)), 1)
    act_across = exchanged(after(joined(act_far, siblings(act_there_far)), grad_across), 1)

    norm_grad, back_stats = call(
        grad_body,
        (f32(tokens, width_part), f32(tokens, 2)),
        (grad_own, siblings(grad_there), grad_across, normal, params),
        "grad",
        flops=6 * tokens * width_part,
    )
    field, direct, handed = call(
        field_body,
        (
            f32(slab_rows, grid_cols, width_part),
            bf16(3, grid_cols, width_part),
            bf16(3, grid_cols, width_part),
        ),
        (norm_grad, back_stats, siblings(back_stats), normal, inverse, params),
        "field",
        scalars=(place,),
        flops=6 * tokens * width_part,
    )
    field_next, field_beyond = neighbours(direct, handed)
    chunks = call(
        terms_body,
        (f32(2, 8, width_part),) * 4,
        (field, next_rows, image, beyond_rows, norm_grad, normal),
        "terms",
        scalars=(place,),
        scratch=[
            shape,
            pltpu.VMEM((slab_rows, grid_cols + 16, 128), jnp.float32),
            pltpu.VMEM((8, 8, width_part), jnp.float32),
        ],
        flops=macs,
    )
    result, *chunks = call(
        result_body,
        (bf16(tokens, width_part), *(f32(2, 8, width_part),) * 4),
        (
            image.reshape(tokens, width_part),
            act_own,
            siblings(act_there),
            act_across,
            flat_cot,
            params,
            *chunks,
        ),
        "result",
        scalars=(place,),
        flops=4 * tokens * width_part,
    )
    total = chunks[0] + exchanged(chunks[1], 1) + exchanged(chunks[2], 2) + exchanged(chunks[3], 3)
    total = total + exchanged(total, 12) + exchanged(total, 8) + exchanged(total, 4)
    totals = (total, exchanged(total, 3), exchanged(total, 2), exchanged(total, 1))
    totals = (totals[0], totals[3], totals[2], totals[1])
    grad_image = call(
        back_body,
        (bf16(slab_rows, grid_cols, width_part),),
        (field_next, after(field, total), field_beyond, kernel, cotangent),
        "back",
        scalars=(place,),
        scratch=[shape, wide],
        flops=macs,
    )[0]
    factor = 1.0 / math.sqrt(tokens * lax.axis_size("row"))
    kernel_sum, param_sum = call(
        functools.partial(final_body, factor),
        (f32(7, 7, width_part), f32(3, width_part)),
        (after(totals[0], grad_image), *totals[1:]),
        "final",
        scalars=(place,),
        scratch=[pltpu.VMEM((8, 8, width_part), jnp.float32)],
    )
    return result.reshape(slab_rows, grid_cols, width_part), grad_image, kernel_sum, param_sum


def padded_2(block, sides, width):
    for axis, dim in sides:
        count = lax.axis_size(axis)
        forward = [(i, i + 1) for i in range(count - 1)]
        backward = [(target, source) for source, target in forward]
        low = lax.ppermute(
            lax.slice_in_dim(block, block.shape[dim] - width, None, axis=dim), axis, forward
        )
        high = lax.ppermute(lax.slice_in_dim(block, 0, width, axis=dim), axis, backward)
        block = jnp.concatenate([low, block, high], axis=dim)
    return block


def depthwise(padded, kernel, height, breadth):
    output = jnp.zeros((height, breadth, kernel.shape[2]), jnp.float32)
    for row_tap in range(7):
        for col_tap in range(7):
            output = (
                output
                + kernel[row_tap, col_tap]
                * padded[row_tap : row_tap + height, col_tap : col_tap + breadth]
            )
    return output


def transposed(padded, kernel, height, breadth):
    output = jnp.zeros((height, breadth, kernel.shape[2]), jnp.float32)
    for row_tap in range(7):
        for col_tap in range(7):
            output = (
                output
                + kernel[row_tap, col_tap]
                * padded[6 - row_tap : 6 - row_tap + height, 6 - col_tap : 6 - col_tap + breadth]
            )
    return output


def gelu_slope(values):
    cumulative = 0.5 * (1.0 + lax.erf(values * (1.0 / math.sqrt(2.0))))
    return cumulative + values * jnp.exp(-0.5 * values * values) * (1.0 / math.sqrt(2.0 * math.pi))


def general(image, kernel, ln_gain, ln_bias, layer_scale, w_in, w_out, cotangent):
    slab_rows, grid_cols, width_part = image.shape
    tokens = slab_rows * grid_cols
    channels = ln_gain.shape[0]
    column = lax.axis_index("col")
    gain_part = lax.dynamic_slice_in_dim(ln_gain, column * width_part, width_part)
    bias_part = lax.dynamic_slice_in_dim(ln_bias, column * width_part, width_part)
    scale_part = lax.dynamic_slice_in_dim(layer_scale, column * width_part, width_part)
    extended = padded_2(image, (("row", 0),), 3)
    padded = jnp.pad(extended.astype(jnp.float32), ((0, 0), (3, 3), (0, 0)))
    conved = depthwise(padded, kernel, slab_rows, grid_cols).reshape(tokens, width_part)
    totals, squares = lax.psum((jnp.sum(conved, axis=1), jnp.sum(conved * conved, axis=1)), "col")
    average = totals / channels
    variance = squares / channels - average * average
    inv_std = lax.rsqrt(variance + epsilon)[:, None]
    normal_part = (conved - average[:, None]) * inv_std
    normed = lax.all_gather(
        (normal_part * gain_part + bias_part).astype(jnp.bfloat16), "col", axis=1, tiled=True
    )
    cot_float = cotangent.reshape(tokens, width_part).astype(jnp.float32)
    scaled = lax.all_gather(
        (cot_float * scale_part).astype(jnp.bfloat16), "col", axis=1, tiled=True
    )
    w_in_all = lax.all_gather(w_in, "row", axis=0, tiled=True)
    w_out_all = lax.all_gather(w_out, "row", axis=1, tiled=True)
    hidden = jnp.dot(normed, w_in_all, preferred_element_type=jnp.float32)
    activated = jax.nn.gelu(hidden, approximate=False).astype(jnp.bfloat16)
    branch_terms = jnp.dot(activated, w_out_all, preferred_element_type=jnp.float32)
    act_grad = jnp.einsum("tc,fc->tf", scaled, w_out_all, preferred_element_type=jnp.float32)
    branch = lax.psum_scatter(branch_terms, "col", scatter_dimension=1, tiled=True)
    result = (image.reshape(tokens, width_part).astype(jnp.float32) + scale_part * branch).astype(
        jnp.bfloat16
    )
    hid_grad = (act_grad * gelu_slope(hidden)).astype(jnp.bfloat16)
    norm_terms = jnp.einsum("tf,cf->tc", hid_grad, w_in_all, preferred_element_type=jnp.float32)
    norm_grad = lax.psum_scatter(norm_terms, "col", scatter_dimension=1, tiled=True)
    grad_hat = norm_grad * gain_part
    first_sum, second_sum = lax.psum(
        (jnp.sum(grad_hat, axis=1), jnp.sum(grad_hat * normal_part, axis=1)), "col"
    )
    conv_grad = inv_std * (
        grad_hat - first_sum[:, None] / channels - normal_part * (second_sum[:, None] / channels)
    )
    grad_field = conv_grad.reshape(slab_rows, grid_cols, width_part)
    grad_extended = padded_2(grad_field, (("row", 0),), 3)
    grad_padded = jnp.pad(grad_extended, ((0, 0), (3, 3), (0, 0)))
    grad_image = (
        cot_float.reshape(slab_rows, grid_cols, width_part)
        + transposed(grad_padded, kernel, slab_rows, grid_cols)
    ).astype(jnp.bfloat16)
    kernel_terms = jnp.stack(
        [
            jnp.stack(
                [
                    jnp.sum(
                        grad_field
                        * padded[row_tap : row_tap + slab_rows, col_tap : col_tap + grid_cols],
                        axis=(0, 1),
                    )
                    for col_tap in range(7)
                ]
            )
            for row_tap in range(7)
        ]
    )
    param_terms = jnp.stack(
        [
            jnp.sum(norm_grad * normal_part, axis=0),
            jnp.sum(norm_grad, axis=0),
            jnp.sum(cot_float * branch, axis=0),
        ]
    )
    kernel_sum, param_sum = lax.psum((kernel_terms, param_terms), "row")
    factor = 1.0 / math.sqrt(tokens * lax.axis_size("row"))
    return (
        result.reshape(slab_rows, grid_cols, width_part),
        grad_image,
        kernel_sum * factor,
        param_sum * factor,
    )


def local(*arguments):
    if lax.axis_size("row") == 16:
        return paired(*arguments)
    return general(*arguments)


def solution(mesh):
    in_specs = (
        P(("groups", "row"), None, "col"),
        P(None, None, "col"),
        P(),
        P(),
        P(),
        P("row", "col"),
        P("col", "row"),
        P(("groups", "row"), None, "col"),
    )
    out_specs = (
        P(("groups", "row"), None, "col"),
        P(("groups", "row"), None, "col"),
        P("groups", None, "col"),
        P("groups", "col"),
    )
    return jax.shard_map(local, mesh=mesh, in_specs=in_specs, out_specs=out_specs, check_vma=False)
```

profile of v0, /device:TPU:0, one launch (start us, length us, event | category | flops | bytes accessed | tf_op | source)
XLA Modules:
  0.0 123.7 jit_solution(17081529480362420400)
XLA Ops:
  0.7 1.2 broadcast_select_fusion
  1.9 3.0 %collective-permute-start.1 = (bf16[3,64,704]{2,1,0:T(8,128)(2,1)S(1)}, bf16[3,64,704]{2,1,0:T(8,128)(2,1)S(1)}, u32[]{:S(2)}, u32[]{:S(2)}) collective-permute-start(bf16[3,64,704]{2,1,0:T(8,128)(2,1)S(1)} %get-tuple-element.102), channel_id=1, source_target_pairs={{0,2},{2,0},{4,6},{6,4},{8,10},{10,8},{12,14},{14,12},{16,18},{18,... | collective-permute-start | bytes 811016 | tf_op jit(solution)/shard_map/ppermute | solution.py:19
  4.9 0.9 fusion.2
  5.8 1.1 fusion.4
  6.9 0.1 concatenate.8
  7.2 2.0 %collective-permute-start.4 = (bf16[88,1408]{1,0:T(8,128)(2,1)S(1)}, bf16[88,1408]{1,0:T(8,128)(2,1)S(1)}, u32[]{:S(2)}, u32[]{:S(2)}) collective-permute-start(bf16[88,1408]{1,0:T(8,128)(2,1)S(1)} %get-tuple-element.58.refs_0_), channel_id=1, source_target_pairs={{0,4},{2,6},{4,0},{6,2},{8,12},{10,14},{12,8},{14,10},{16,20},{18,... | collective-permute-start | bytes 743432 | tf_op jit(solution)/shard_map/ppermute | solution.py:19
  9.3 1.5 %collective-permute-start = (bf16[3,64,704]{2,1,0:T(8,128)(2,1)S(1)}, bf16[3,64,704]{2,1,0:T(8,128)(2,1)S(1)}, u32[]{:S(2)}, u32[]{:S(2)}) collective-permute-start(bf16[3,64,704]{2,1,0:T(8,128)(2,1)S(1)} %get-tuple-element.103), channel_id=1, source_target_pairs={{0,2},{2,0},{4,6},{6,4},{8,10},{10,8},{12,14},{14,12},{16,18},{18,... | collective-permute-start | bytes 811016 | tf_op jit(solution)/shard_map/ppermute | solution.py:19
  10.8 2.6 %collective-permute-start.11 = (bf16[88,1408]{1,0:T(8,128)(2,1)S(1)}, bf16[88,1408]{1,0:T(8,128)(2,1)S(1)}, u32[]{:S(2)}, u32[]{:S(2)}) collective-permute-start(bf16[88,1408]{1,0:T(8,128)(2,1)S(1)} %get-tuple-element.58.refs_0_), channel_id=1, source_target_pairs={{0,16},{2,18},{4,20},{6,22},{8,24},{10,26},{12,28},{14,30},{16,0},... | collective-permute-start | bytes 743432 | tf_op jit(solution)/shard_map/ppermute | solution.py:19
  13.6 4.4 %collective-permute-done.3.refs_8_ = bf16[88,1408]{1,0:T(8,128)(2,1)S(1)} collective-permute-done((bf16[88,1408]{1,0:T(8,128)(2,1)S(1)}, bf16[88,1408]{1,0:T(8,128)(2,1)S(1)}, u32[]{:S(2)}, u32[]{:S(2)}) %collective-permute-start.3) | collective-permute-done | bytes 247840 | tf_op jit(solution)/shard_map/ppermute | solution.py:19
  18.0 2.1 %collective-permute-start.8 = (bf16[88,1408]{1,0:T(8,128)(2,1)S(1)}, bf16[88,1408]{1,0:T(8,128)(2,1)S(1)}, u32[]{:S(2)}, u32[]{:S(2)}) collective-permute-start(bf16[88,1408]{1,0:T(8,128)(2,1)S(1)} %get-tuple-element.58.refs_0_), channel_id=1, source_target_pairs={{0,8},{2,10},{4,12},{6,14},{8,0},{10,2},{12,4},{14,6},{16,24},{18,... | collective-permute-start | bytes 743432 | tf_op jit(solution)/shard_map/ppermute | solution.py:19
  20.2 1.5 %collective-permute-start.9 = (bf16[88,1408]{1,0:T(8,128)(2,1)S(1)}, bf16[88,1408]{1,0:T(8,128)(2,1)S(1)}, u32[]{:S(2)}, u32[]{:S(2)}) collective-permute-start(bf16[88,1408]{1,0:T(8,128)(2,1)S(1)} %collective-permute-done.3.refs_8_), channel_id=1, source_target_pairs={{0,4},{2,6},{4,0},{6,2},{8,12},{10,14},{12,8},{14,10},{16,20},{18,... | collective-permute-start | bytes 743432 | tf_op jit(solution)/shard_map/ppermute | solution.py:19
  21.7 2.4 %collective-permute-start.2 = (bf16[3,64,704]{2,1,0:T(8,128)(2,1)S(1)}, bf16[3,64,704]{2,1,0:T(8,128)(2,1)S(1)}, u32[]{:S(2)}, u32[]{:S(2)}) collective-permute-start(bf16[3,64,704]{2,1,0:T(8,128)(2,1)S(1)} %collective-permute-done.1), channel_id=1, source_target_pairs={{0,4},{4,8},{8,12},{12,16},{16,20},{20,24},{24,28},{6,2},{10,6},{1... | collective-permute-start | bytes 811016 | tf_op jit(solution)/shard_map/ppermute | solution.py:49
  24.3 2.6 %collective-permute-start.16 = (bf16[88,1408]{1,0:T(8,128)(2,1)S(1)}, bf16[88,1408]{1,0:T(8,128)(2,1)S(1)}, u32[]{:S(2)}, u32[]{:S(2)}) collective-permute-start(bf16[88,1408]{1,0:T(8,128)(2,1)S(1)} %collective-permute-done.3.refs_8_), channel_id=1, source_target_pairs={{0,16},{2,18},{4,20},{6,22},{8,24},{10,26},{12,28},{14,30},{16,0},... | collective-permute-start | bytes 743432 | tf_op jit(solution)/shard_map/ppermute | solution.py:19
  26.9 3.6 %collective-permute-done.8.refs_2_ = bf16[88,1408]{1,0:T(8,128)(2,1)S(1)} collective-permute-done((bf16[88,1408]{1,0:T(8,128)(2,1)S(1)}, bf16[88,1408]{1,0:T(8,128)(2,1)S(1)}, u32[]{:S(2)}, u32[]{:S(2)}) %collective-permute-start.8) | collective-permute-done | bytes 247840 | tf_op jit(solution)/shard_map/ppermute | solution.py:19
  30.6 2.0 %collective-permute-start.10 = (bf16[88,1408]{1,0:T(8,128)(2,1)S(1)}, bf16[88,1408]{1,0:T(8,128)(2,1)S(1)}, u32[]{:S(2)}, u32[]{:S(2)}) collective-permute-start(bf16[88,1408]{1,0:T(8,128)(2,1)S(1)} %collective-permute-done.8.refs_2_), channel_id=1, source_target_pairs={{0,4},{2,6},{4,0},{6,2},{8,12},{10,14},{12,8},{14,10},{16,20},{18,... | collective-permute-start | bytes 743432 | tf_op jit(solution)/shard_map/ppermute | solution.py:19
  32.6 3.6 %conv.1 = (f32[256,704]{1,0:T(8,128)S(1)}, f32[256,2]{1,0:T(8,128)S(1)}) custom-call(s32[2]{0:T(128)S(1)} %pad_add_fusion.place, bf16[3,64,704]{2,1,0:T(8,128)(2,1)S(1)} %collective-permute-done.near, bf16[4,64,704]{2,1,0:T(8,128)(2,1)S(1)} %copy-done.1, bf16[3,64,704]{2,1,0:T(8,128)(2,1)S(1)} %collective-permute-done.2.beyond, f32[7,7,704]{2,1,0:T(8,128)S(1)} %copy-done.2), custom_call_target="tpu_custom_call" | custom-call | flops 17661952000 | bytes 1762048 | tf_op jit(solution)/shard_map/conv/pallas_call | solution.py:54
  36.4 2.5 %collective-permute-start.7 = (bf16[4,64,704]{2,1,0:T(8,128)(2,1)S(1)}, bf16[4,64,704]{2,1,0:T(8,128)(2,1)S(1)}, u32[]{:S(2)}, u32[]{:S(2)}) collective-permute-start(bf16[4,64,704]{2,1,0:T(8,128)(2,1)S(1)} %bitcast.51), channel_id=1, source_target_pairs={{0,2},{2,0},{4,6},{6,4},{8,10},{10,8},{12,14},{14,12},{16,18},{18,... | collective-permute-start | bytes 1081352 | tf_op jit(solution)/shard_map/ppermute | solution.py:18
  38.9 5.6 %collective-permute-start.12 = (bf16[88,1408]{1,0:T(8,128)(2,1)S(1)}, bf16[88,1408]{1,0:T(8,128)(2,1)S(1)}, u32[]{:S(2)}, u32[]{:S(2)}) collective-permute-start(bf16[88,1408]{1,0:T(8,128)(2,1)S(1)} %collective-permute-done.11.refs_4_), channel_id=1, source_target_pairs={{0,4},{2,6},{4,0},{6,2},{8,12},{10,14},{12,8},{14,10},{16,20},{18,... | collective-permute-start | bytes 743432 | tf_op jit(solution)/shard_map/ppermute | solution.py:19
  44.5 0.1 collective-permute-start.19
  44.6 2.4 %all-gather.1 = bf16[8,64,704]{2,1,0:T(8,128)(2,1)S(1)} all-gather(bf16[4,64,704]{2,1,0:T(8,128)(2,1)S(1)} %multiply_convert_fusion.1), channel_id=3, replica_groups=mesh['groups'=1,'row'=16,'col'=2] {'col'}, dimensions={0}, use_global_device_ids=true | all-gather | bytes 1081344 | tf_op jit(solution)/shard_map/all_gather | solution.py:33
  47.0 0.3 norm.1
  47.3 1.1 collective-permute-start.6
  48.3 2.4 %all_gather.12 = bf16[2,4,64,704]{3,2,1,0:T(8,128)(2,1)S(1)} all-gather(bf16[1,4,64,704]{3,2,1,0:T(8,128)(2,1)S(1)} %bitcast.39), channel_id=1, replica_groups=mesh['groups'=1,'row'=16,'col'=2] {'col'}, dimensions={0}, use_global_device_ids=true | all-gather | bytes 1081344 | tf_op jit(solution)/shard_map/all_gather | solution.py:33
  50.7 0.5 collective-permute-done.12.refs_5_
  51.2 2.1 %collective-permute-start.14 = (bf16[88,1408]{1,0:T(8,128)(2,1)S(1)}, bf16[88,1408]{1,0:T(8,128)(2,1)S(1)}, u32[]{:S(2)}, u32[]{:S(2)}) collective-permute-start(bf16[88,1408]{1,0:T(8,128)(2,1)S(1)} %collective-permute-done.13.refs_6_), channel_id=1, source_target_pairs={{0,4},{2,6},{4,0},{6,2},{8,12},{10,14},{12,8},{14,10},{16,20},{18,... | collective-permute-start | bytes 743432 | tf_op jit(solution)/shard_map/ppermute | solution.py:19
  53.3 0.4 collective-permute-start.15
  53.7 2.9 %collective-permute-done.19.refs_13_ = bf16[88,1408]{1,0:T(8,128)(2,1)S(1)} collective-permute-done((bf16[88,1408]{1,0:T(8,128)(2,1)S(1)}, bf16[88,1408]{1,0:T(8,128)(2,1)S(1)}, u32[]{:S(2)}, u32[]{:S(2)}) %collective-permute-start.19) | collective-permute-done | bytes 247840 | tf_op jit(solution)/shard_map/ppermute | solution.py:19
  56.5 2.1 %collective-permute-start.20 = (bf16[88,1408]{1,0:T(8,128)(2,1)S(1)}, bf16[88,1408]{1,0:T(8,128)(2,1)S(1)}, u32[]{:S(2)}, u32[]{:S(2)}) collective-permute-start(bf16[88,1408]{1,0:T(8,128)(2,1)S(1)} %collective-permute-done.17.refs_14_), channel_id=1, source_target_pairs={{0,4},{2,6},{4,0},{6,2},{8,12},{10,14},{12,8},{14,10},{16,20},{18,... | collective-permute-start | bytes 743432 | tf_op jit(solution)/shard_map/ppermute | solution.py:19
  58.6 2.4 %all-gather.2 = bf16[8,64,704]{2,1,0:T(8,128)(2,1)S(1)} all-gather(bf16[4,64,704]{2,1,0:T(8,128)(2,1)S(1)} %collective-permute-done.7), channel_id=4, replica_groups=mesh['groups'=1,'row'=16,'col'=2] {'col'}, dimensions={0}, use_global_device_ids=true | all-gather | bytes 1081344 | tf_op jit(solution)/shard_map/all_gather | solution.py:33
  61.0 2.4 %all-gather = bf16[8,64,704]{2,1,0:T(8,128)(2,1)S(1)} all-gather(bf16[4,64,704]{2,1,0:T(8,128)(2,1)S(1)} %collective-permute-done.6), channel_id=2, replica_groups=mesh['groups'=1,'row'=16,'col'=2] {'col'}, dimensions={0}, use_global_device_ids=true | all-gather | bytes 1081344 | tf_op jit(solution)/shard_map/all_gather | solution.py:33
  63.3 1.7 %collective-permute-done.18.refs_11_ = bf16[88,1408]{1,0:T(8,128)(2,1)S(1)} collective-permute-done((bf16[88,1408]{1,0:T(8,128)(2,1)S(1)}, bf16[88,1408]{1,0:T(8,128)(2,1)S(1)}, u32[]{:S(2)}, u32[]{:S(2)}) %collective-permute-start.18) | collective-permute-done | bytes 247840 | tf_op jit(solution)/shard_map/ppermute | solution.py:19
  65.0 1.7 %collective-permute-done.20.refs_15_ = bf16[88,1408]{1,0:T(8,128)(2,1)S(1)} collective-permute-done((bf16[88,1408]{1,0:T(8,128)(2,1)S(1)}, bf16[88,1408]{1,0:T(8,128)(2,1)S(1)}, u32[]{:S(2)}, u32[]{:S(2)}) %collective-permute-start.20) | collective-permute-done | bytes 247840 | tf_op jit(solution)/shard_map/ppermute | solution.py:19
  66.7 4.8 %mlp.1 = (f32[256,704]{1,0:T(8,128)S(1)}, f32[256,704]{1,0:T(8,128)S(1)}, f32[256,704]{1,0:T(8,128)S(1)}, f32[256,704]{1,0:T(8,128)S(1)}, bf16[1408,1408]{1,0:T(8,128)(2,1)S(1)}, /*index=5*/bf16[512,768]{1,0:T(8,128)(2,1)S(1)}) custom-call(s32[2]{0:T(128)S(1)} %pad_add_fusion.place, bf16[2,256,704]{2,1,0:T(8,128)(2,1)S(1)} %bitcast.30, ...), custom_call_target="tpu_custom_call" | custom-call | flops 3045064704 | bytes 14483456 | tf_op jit(solution)/shard_map/mlp/pallas_call | solution.py:54
  71.6 1.4 %branch.1 = (f32[256,704]{1,0:T(8,128)S(1)}, f32[256,704]{1,0:T(8,128)S(1)}, f32[256,704]{1,0:T(8,128)S(1)}, f32[256,704]{1,0:T(8,128)S(1)}) custom-call(bf16[512,768]{1,0:T(8,128)(2,1)S(1)} %get-tuple-element.69.act, bf16[1408,1408]{1,0:T(8,128)(2,1)S(1)} %get-tuple-element.70.whole), custom_call_target="tpu_custom_call" | custom-call | flops 1015021568 | bytes 7634944 | tf_op jit(solution)/shard_map/branch/pallas_call | solution.py:54
  73.0 0.6 collective-permute-start.22
  73.7 0.2 collective-permute-done.23
  73.9 0.4 collective-permute-start.24
  74.4 1.1 collective-permute-done.22
  75.6 9.7 %collective-permute-done.24 = bf16[4,64,704]{2,1,0:T(8,128)(2,1)S(1)} collective-permute-done((bf16[4,64,704]{2,1,0:T(8,128)(2,1)S(1)}, bf16[4,64,704]{2,1,0:T(8,128)(2,1)S(1)}, u32[]{:S(2)}, u32[]{:S(2)}) %collective-permute-start.24) | collective-permute-done | bytes 360480 | tf_op jit(solution)/shard_map/ppermute | solution.py:18
  85.2 0.4 collective-permute-start.25
  85.6 0.4 grad.1
  86.0 1.3 %collective-permute-done.27.other = f32[256,2]{1,0:T(8,128)S(1)} collective-permute-done((f32[256,2]{1,0:T(8,128)S(1)}, f32[256,2]{1,0:T(8,128)S(1)}, u32[]{:S(2)}, u32[]{:S(2)}) %collective-permute-start.27) | collective-permute-done | bytes 2080 | tf_op jit(solution)/shard_map/ppermute | solution.py:19
  87.4 0.9 field.1
  88.2 4.5 %terms.1 = (f32[2,8,704]{2,1,0:T(8,128)S(1)}, f32[2,8,704]{2,1,0:T(8,128)S(1)}, f32[2,8,704]{2,1,0:T(8,128)S(1)}, f32[2,8,704]{2,1,0:T(8,128)S(1)}) custom-call(s32[2]{0:T(128)S(1)} %pad_add_fusion.place, f32[4,64,704]{2,1,0:T(8,128)S(1)} %get-tuple-element.95.field.middle, bf16[3,64,704]{2,1,0:T(8,128)(2,1)S(1)} %collective-permute-done.near, ...), custom_call_target="tpu_custom_call" | custom-call | flops 17661952 | bytes 3244032 | tf_op jit(solution)/shard_map/terms/pallas_call | solution.py:54
  92.8 2.9 %collective-permute-done.25 = bf16[4,64,704]{2,1,0:T(8,128)(2,1)S(1)} collective-permute-done((bf16[4,64,704]{2,1,0:T(8,128)(2,1)S(1)}, bf16[4,64,704]{2,1,0:T(8,128)(2,1)S(1)}, u32[]{:S(2)}, u32[]{:S(2)}) %collective-permute-start.25) | collective-permute-done | bytes 360480 | tf_op jit(solution)/shard_map/ppermute | solution.py:18
  95.7 1.6 %result.1 = (bf16[256,704]{1,0:T(8,128)(2,1)}, f32[2,8,704]{2,1,0:T(8,128)S(1)}, f32[2,8,704]{2,1,0:T(8,128)S(1)}, f32[2,8,704]{2,1,0:T(8,128)S(1)}, f32[2,8,704]{2,1,0:T(8,128)S(1)}) custom-call(s32[2]{0:T(128)S(1)} %pad_add_fusion.place, bf16[256,704]{1,0:T(8,128)(2,1)S(1)} %bitcast.28, f32[256,704]{1,0:T(8,128)S(1)} %get-tuple-element.71.mine, ...), custom_call_target="tpu_custom_call" | custom-call | flops 720896 | bytes 3252480 | tf_op jit(solution)/shard_map/result/pallas_call | solution.py:54
  97.3 0.4 collective-permute-start.29
  97.7 1.7 %collective-permute-start.30 = (f32[2,8,704]{2,1,0:T(8,128)S(1)}, f32[2,8,704]{2,1,0:T(8,128)S(1)}, u32[]{:S(2)}, u32[]{:S(2)}) collective-permute-start(f32[2,8,704]{2,1,0:T(8,128)S(1)} %get-tuple-element.93), channel_id=1, source_target_pairs={{0,4},{2,6},{4,0},{6,2},{8,12},{10,14},{12,8},{14,10},{16,20},{18,... | collective-permute-start | bytes 135176 | tf_op jit(solution)/shard_map/ppermute | solution.py:19
  99.4 1.4 %collective-permute-start.31 = (f32[2,8,704]{2,1,0:T(8,128)S(1)}, f32[2,8,704]{2,1,0:T(8,128)S(1)}, u32[]{:S(2)}, u32[]{:S(2)}) collective-permute-start(f32[2,8,704]{2,1,0:T(8,128)S(1)} %get-tuple-element.94), channel_id=1, source_target_pairs={{0,6},{2,4},{4,2},{6,0},{8,14},{10,12},{12,10},{14,8},{16,22},{18,... | collective-permute-start | bytes 135176 | tf_op jit(solution)/shard_map/ppermute | solution.py:19
  100.8 0.4 collective-permute-start.35
  101.1 0.6 collective-permute-done.29
  101.7 0.2 collective-permute-done.30
  101.9 3.0 %collective-permute-done.31 = f32[2,8,704]{2,1,0:T(8,128)S(1)} collective-permute-done((f32[2,8,704]{2,1,0:T(8,128)S(1)}, f32[2,8,704]{2,1,0:T(8,128)S(1)}, u32[]{:S(2)}, u32[]{:S(2)}) %collective-permute-start.31) | collective-permute-done | bytes 45088 | tf_op jit(solution)/shard_map/ppermute | solution.py:19
  105.0 0.3 collective-permute-start.34
  105.3 3.6 %collective-permute-start.33 = (f32[2,8,704]{2,1,0:T(8,128)S(1)}, f32[2,8,704]{2,1,0:T(8,128)S(1)}, u32[]{:S(2)}, u32[]{:S(2)}) collective-permute-start(f32[2,8,704]{2,1,0:T(8,128)S(1)} %add_add_fusion.1), channel_id=1, source_target_pairs={{0,16},{2,18},{4,20},{6,22},{8,24},{10,26},{12,28},{14,30},{16,0},... | collective-permute-start | bytes 135176 | tf_op jit(solution)/shard_map/ppermute | solution.py:19
  108.8 0.6 collective-permute-start.32
  109.4 1.7 %collective-permute-start.28 = (bf16[3,64,704]{2,1,0:T(8,128)(2,1)S(1)}, bf16[3,64,704]{2,1,0:T(8,128)(2,1)S(1)}, u32[]{:S(2)}, u32[]{:S(2)}) collective-permute-start(bf16[3,64,704]{2,1,0:T(8,128)(2,1)S(1)} %get-tuple-element.90), channel_id=1, source_target_pairs={{0,2},{2,0},{4,6},{6,4},{8,10},{10,8},{12,14},{14,12},{16,18},{18,... | collective-permute-start | bytes 811016 | tf_op jit(solution)/shard_map/ppermute | solution.py:19
  111.1 2.2 %collective-permute-start.36 = (bf16[3,64,704]{2,1,0:T(8,128)(2,1)S(1)}, bf16[3,64,704]{2,1,0:T(8,128)(2,1)S(1)}, u32[]{:S(2)}, u32[]{:S(2)}) collective-permute-start(bf16[3,64,704]{2,1,0:T(8,128)(2,1)S(1)} %collective-permute-done.35), channel_id=1, source_target_pairs={{0,4},{4,8},{8,12},{12,16},{16,20},{20,24},{24,28},{6,2},{10,6},{1... | collective-permute-start | bytes 811016 | tf_op jit(solution)/shard_map/ppermute | solution.py:49
  113.3 1.4 %collective-permute-done.32 = f32[2,8,704]{2,1,0:T(8,128)S(1)} collective-permute-done((f32[2,8,704]{2,1,0:T(8,128)S(1)}, f32[2,8,704]{2,1,0:T(8,128)S(1)}, u32[]{:S(2)}, u32[]{:S(2)}) %collective-permute-start.32) | collective-permute-done | bytes 45088 | tf_op jit(solution)/shard_map/ppermute | solution.py:19
  114.7 1.6 %collective-permute-start.39 = (f32[2,8,704]{2,1,0:T(8,128)S(1)}, f32[2,8,704]{2,1,0:T(8,128)S(1)}, u32[]{:S(2)}, u32[]{:S(2)}) collective-permute-start(f32[2,8,704]{2,1,0:T(8,128)S(1)} %add_add_fusion.c0), channel_id=1, source_target_pairs={{0,6},{2,4},{4,2},{6,0},{8,14},{10,12},{12,10},{14,8},{16,22},{18,... | collective-permute-start | bytes 135176 | tf_op jit(solution)/shard_map/ppermute | solution.py:19
  116.3 0.8 collective-permute-start.38
  117.1 1.2 collective-permute-start.37
  118.3 4.1 %back.1 = bf16[4,64,704]{2,1,0:T(8,128)(2,1)} custom-call(s32[2]{0:T(128)S(1)} %pad_add_fusion.place, bf16[3,64,704]{2,1,0:T(8,128)(2,1)S(1)} %collective-permute-done.28.near, f32[4,64,704]{2,1,0:T(8,128)S(1)} %get-tuple-element.95.field.middle, bf16[3,64,704]{2,1,0:T(8,128)(2,1)S(1)} %collective-permute-done.36.beyond, f32[7,7,704]{2,1,0:T(8,128)S(1)} %copy-done.2, ...), custom_call_target="tpu_custom_call" | custom-call | flops 17661952 | bytes 2120448 | tf_op jit(solution)/shard_map/back/pallas_call | solution.py:54
  122.4 1.2 %final.1 = (f32[7,7,704]{2,1,0:T(8,128)}, f32[3,704]{1,0:T(4,128)}) custom-call(s32[2]{0:T(128)S(1)} %pad_add_fusion.place, f32[2,8,704]{2,1,0:T(8,128)S(1)} %add_add_fusion.c0, f32[2,8,704]{2,1,0:T(8,128)S(1)} %collective-permute-done.37.c1, f32[2,8,704]{2,1,0:T(8,128)S(1)} %collective-permute-done.38.c2, f32[2,8,704]{2,1,0:T(8,128)S(1)} %collective-permute-done.39.c3), custom_call_target="tpu_custom_call" | custom-call | bytes 326656 | tf_op jit(solution)/shard_map/final/pallas_call | solution.py:54
  (60 shorter events, 1.3 us)
Async XLA Ops:
  0.6 31.9 %copy-start.1 = (bf16[4,64,704]{2,1,0:T(8,128)(2,1)S(1)}, bf16[4,64,704]{2,1,0:T(8,128)(2,1)}, u32[]{:S(2)}) copy-start(bf16[4,64,704]{2,1,0:T(8,128)(2,1)} %middle.3) | copy-start | bytes 1081348
  0.6 12.7 %copy-start.3 = (f32[1408]{0:T(1024)S(1)}, f32[1408]{0:T(1024)}, u32[]{:S(2)}) copy-start(f32[1408]{0:T(1024)} %param.10) | copy-start | bytes 16900
  0.7 12.8 %copy-start.4 = (f32[1408]{0:T(1024)S(1)}, f32[1408]{0:T(1024)}, u32[]{:S(2)}) copy-start(f32[1408]{0:T(1024)} %param.11) | copy-start | bytes 16900
  0.7 12.8 %copy-start.5 = (f32[1408]{0:T(1024)S(1)}, f32[1408]{0:T(1024)}, u32[]{:S(2)}) copy-start(f32[1408]{0:T(1024)} %param.12) | copy-start | bytes 16900
  0.7 23.5 %copy-start = (bf16[4,64,704]{2,1,0:T(8,128)(2,1)S(1)}, bf16[4,64,704]{2,1,0:T(8,128)(2,1)}, u32[]{:S(2)}) copy-start(bf16[4,64,704]{2,1,0:T(8,128)(2,1)} %cot.1) | copy-start | bytes 1081348
  0.7 31.9 %copy-start.2 = (f32[7,7,704]{2,1,0:T(8,128)S(1)}, f32[7,7,704]{2,1,0:T(8,128)}, u32[]{:S(2)}) copy-start(f32[7,7,704]{2,1,0:T(8,128)} %kernel.3) | copy-start | bytes 413956
  1.9 19.8 %collective-permute-start.1 = (bf16[3,64,704]{2,1,0:T(8,128)(2,1)S(1)}, bf16[3,64,704]{2,1,0:T(8,128)(2,1)S(1)}, u32[]{:S(2)}, u32[]{:S(2)}) collective-permute-start(bf16[3,64,704]{2,1,0:T(8,128)(2,1)S(1)} %get-tuple-element.102), channel_id=1, source_target_pairs={{0,2},{2,0},{4,6},{6,4},{8,10},{10,8},{12,14},{14,12},{16,18},{18,... | collective-permute-start | bytes 811016 | tf_op jit(solution)/shard_map/ppermute | solution.py:19
  7.1 10.9 %collective-permute-start.3 = (bf16[88,1408]{1,0:T(8,128)(2,1)S(1)}, bf16[88,1408]{1,0:T(8,128)(2,1)S(1)}, u32[]{:S(2)}, u32[]{:S(2)}) collective-permute-start(bf16[88,1408]{1,0:T(8,128)(2,1)S(1)} %get-tuple-element.101), channel_id=1, source_target_pairs={{0,2},{2,0},{4,6},{6,4},{8,10},{10,8},{12,14},{14,12},{16,18},{18,... | collective-permute-start | bytes 743432 | tf_op jit(solution)/shard_map/ppermute | solution.py:19
  7.2 10.8 %collective-permute-start.4 = (bf16[88,1408]{1,0:T(8,128)(2,1)S(1)}, bf16[88,1408]{1,0:T(8,128)(2,1)S(1)}, u32[]{:S(2)}, u32[]{:S(2)}) collective-permute-start(bf16[88,1408]{1,0:T(8,128)(2,1)S(1)} %get-tuple-element.58.refs_0_), channel_id=1, source_target_pairs={{0,4},{2,6},{4,0},{6,2},{8,12},{10,14},{12,8},{14,10},{16,20},{18,... | collective-permute-start | bytes 743432 | tf_op jit(solution)/shard_map/ppermute | solution.py:19
  9.3 23.3 %collective-permute-start = (bf16[3,64,704]{2,1,0:T(8,128)(2,1)S(1)}, bf16[3,64,704]{2,1,0:T(8,128)(2,1)S(1)}, u32[]{:S(2)}, u32[]{:S(2)}) collective-permute-start(bf16[3,64,704]{2,1,0:T(8,128)(2,1)S(1)} %get-tuple-element.103), channel_id=1, source_target_pairs={{0,2},{2,0},{4,6},{6,4},{8,10},{10,8},{12,14},{14,12},{16,18},{18,... | collective-permute-start | bytes 811016 | tf_op jit(solution)/shard_map/ppermute | solution.py:19
  10.8 13.5 %collective-permute-start.11 = (bf16[88,1408]{1,0:T(8,128)(2,1)S(1)}, bf16[88,1408]{1,0:T(8,128)(2,1)S(1)}, u32[]{:S(2)}, u32[]{:S(2)}) collective-permute-start(bf16[88,1408]{1,0:T(8,128)(2,1)S(1)} %get-tuple-element.58.refs_0_), channel_id=1, source_target_pairs={{0,16},{2,18},{4,20},{6,22},{8,24},{10,26},{12,28},{14,30},{16,0},... | collective-permute-start | bytes 743432 | tf_op jit(solution)/shard_map/ppermute | solution.py:19
  18.0 12.5 %collective-permute-start.8 = (bf16[88,1408]{1,0:T(8,128)(2,1)S(1)}, bf16[88,1408]{1,0:T(8,128)(2,1)S(1)}, u32[]{:S(2)}, u32[]{:S(2)}) collective-permute-start(bf16[88,1408]{1,0:T(8,128)(2,1)S(1)} %get-tuple-element.58.refs_0_), channel_id=1, source_target_pairs={{0,8},{2,10},{4,12},{6,14},{8,0},{10,2},{12,4},{14,6},{16,24},{18,... | collective-permute-start | bytes 743432 | tf_op jit(solution)/shard_map/ppermute | solution.py:19
  20.2 10.4 %collective-permute-start.9 = (bf16[88,1408]{1,0:T(8,128)(2,1)S(1)}, bf16[88,1408]{1,0:T(8,128)(2,1)S(1)}, u32[]{:S(2)}, u32[]{:S(2)}) collective-permute-start(bf16[88,1408]{1,0:T(8,128)(2,1)S(1)} %collective-permute-done.3.refs_8_), channel_id=1, source_target_pairs={{0,4},{2,6},{4,0},{6,2},{8,12},{10,14},{12,8},{14,10},{16,20},{18,... | collective-permute-start | bytes 743432 | tf_op jit(solution)/shard_map/ppermute | solution.py:19
  21.7 10.9 %collective-permute-start.2 = (bf16[3,64,704]{2,1,0:T(8,128)(2,1)S(1)}, bf16[3,64,704]{2,1,0:T(8,128)(2,1)S(1)}, u32[]{:S(2)}, u32[]{:S(2)}) collective-permute-start(bf16[3,64,704]{2,1,0:T(8,128)(2,1)S(1)} %collective-permute-done.1), channel_id=1, source_target_pairs={{0,4},{4,8},{8,12},{12,16},{16,20},{20,24},{24,28},{6,2},{10,6},{1... | collective-permute-start | bytes 811016 | tf_op jit(solution)/shard_map/ppermute | solution.py:49
  24.3 14.6 %collective-permute-start.16 = (bf16[88,1408]{1,0:T(8,128)(2,1)S(1)}, bf16[88,1408]{1,0:T(8,128)(2,1)S(1)}, u32[]{:S(2)}, u32[]{:S(2)}) collective-permute-start(bf16[88,1408]{1,0:T(8,128)(2,1)S(1)} %collective-permute-done.3.refs_8_), channel_id=1, source_target_pairs={{0,16},{2,18},{4,20},{6,22},{8,24},{10,26},{12,28},{14,30},{16,0},... | collective-permute-start | bytes 743432 | tf_op jit(solution)/shard_map/ppermute | solution.py:19
  30.6 16.7 %collective-permute-start.13 = (bf16[88,1408]{1,0:T(8,128)(2,1)S(1)}, bf16[88,1408]{1,0:T(8,128)(2,1)S(1)}, u32[]{:S(2)}, u32[]{:S(2)}) collective-permute-start(bf16[88,1408]{1,0:T(8,128)(2,1)S(1)} %collective-permute-done.11.refs_4_), channel_id=1, source_target_pairs={{0,8},{2,10},{4,12},{6,14},{8,0},{10,2},{12,4},{14,6},{16,24},{18,... | collective-permute-start | bytes 743432 | tf_op jit(solution)/shard_map/ppermute | solution.py:19
  30.6 13.9 %collective-permute-start.10 = (bf16[88,1408]{1,0:T(8,128)(2,1)S(1)}, bf16[88,1408]{1,0:T(8,128)(2,1)S(1)}, u32[]{:S(2)}, u32[]{:S(2)}) collective-permute-start(bf16[88,1408]{1,0:T(8,128)(2,1)S(1)} %collective-permute-done.8.refs_2_), channel_id=1, source_target_pairs={{0,4},{2,6},{4,0},{6,2},{8,12},{10,14},{12,8},{14,10},{16,20},{18,... | collective-permute-start | bytes 743432 | tf_op jit(solution)/shard_map/ppermute | solution.py:19
  36.2 8.2 %collective-permute-start.5 = (f32[256,2]{1,0:T(8,128)S(1)}, f32[256,2]{1,0:T(8,128)S(1)}, u32[]{:S(2)}, u32[]{:S(2)}) collective-permute-start(f32[256,2]{1,0:T(8,128)S(1)} %get-tuple-element.55.mine), channel_id=1, source_target_pairs={{0,1},{1,0},{2,3},{3,2},{4,5},{5,4},{6,7},{7,6},{8,9},{9,8},{10,11... | collective-permute-start | bytes 6152 | tf_op jit(solution)/shard_map/ppermute | solution.py:19
  36.4 20.2 %collective-permute-start.7 = (bf16[4,64,704]{2,1,0:T(8,128)(2,1)S(1)}, bf16[4,64,704]{2,1,0:T(8,128)(2,1)S(1)}, u32[]{:S(2)}, u32[]{:S(2)}) collective-permute-start(bf16[4,64,704]{2,1,0:T(8,128)(2,1)S(1)} %bitcast.51), channel_id=1, source_target_pairs={{0,2},{2,0},{4,6},{6,4},{8,10},{10,8},{12,14},{14,12},{16,18},{18,... | collective-permute-start | bytes 1081352 | tf_op jit(solution)/shard_map/ppermute | solution.py:18
  38.9 12.3 %collective-permute-start.12 = (bf16[88,1408]{1,0:T(8,128)(2,1)S(1)}, bf16[88,1408]{1,0:T(8,128)(2,1)S(1)}, u32[]{:S(2)}, u32[]{:S(2)}) collective-permute-start(bf16[88,1408]{1,0:T(8,128)(2,1)S(1)} %collective-permute-done.11.refs_4_), channel_id=1, source_target_pairs={{0,4},{2,6},{4,0},{6,2},{8,12},{10,14},{12,8},{14,10},{16,20},{18,... | collective-permute-start | bytes 743432 | tf_op jit(solution)/shard_map/ppermute | solution.py:19
  44.5 8.8 %collective-permute-start.17 = (bf16[88,1408]{1,0:T(8,128)(2,1)S(1)}, bf16[88,1408]{1,0:T(8,128)(2,1)S(1)}, u32[]{:S(2)}, u32[]{:S(2)}) collective-permute-start(bf16[88,1408]{1,0:T(8,128)(2,1)S(1)} %collective-permute-done.16.refs_12_), channel_id=1, source_target_pairs={{0,8},{2,10},{4,12},{6,14},{8,0},{10,2},{12,4},{14,6},{16,24},{18,... | collective-permute-start | bytes 743432 | tf_op jit(solution)/shard_map/ppermute | solution.py:19
  44.5 12.1 %collective-permute-start.19 = (bf16[88,1408]{1,0:T(8,128)(2,1)S(1)}, bf16[88,1408]{1,0:T(8,128)(2,1)S(1)}, u32[]{:S(2)}, u32[]{:S(2)}) collective-permute-start(bf16[88,1408]{1,0:T(8,128)(2,1)S(1)} %collective-permute-done.16.refs_12_), channel_id=1, source_target_pairs={{0,4},{2,6},{4,0},{6,2},{8,12},{10,14},{12,8},{14,10},{16,20},{18,... | collective-permute-start | bytes 743432 | tf_op jit(solution)/shard_map/ppermute | solution.py:19
  47.3 13.7 %collective-permute-start.6 = (bf16[4,64,704]{2,1,0:T(8,128)(2,1)S(1)}, bf16[4,64,704]{2,1,0:T(8,128)(2,1)S(1)}, u32[]{:S(2)}, u32[]{:S(2)}) collective-permute-start(bf16[4,64,704]{2,1,0:T(8,128)(2,1)S(1)} %bitcast.38), channel_id=1, source_target_pairs={{0,2},{2,0},{4,6},{6,4},{8,10},{10,8},{12,14},{14,12},{16,18},{18,... | collective-permute-start | bytes 1081352 | tf_op jit(solution)/shard_map/ppermute | solution.py:18
  51.2 12.1 %collective-permute-start.14 = (bf16[88,1408]{1,0:T(8,128)(2,1)S(1)}, bf16[88,1408]{1,0:T(8,128)(2,1)S(1)}, u32[]{:S(2)}, u32[]{:S(2)}) collective-permute-start(bf16[88,1408]{1,0:T(8,128)(2,1)S(1)} %collective-permute-done.13.refs_6_), channel_id=1, source_target_pairs={{0,4},{2,6},{4,0},{6,2},{8,12},{10,14},{12,8},{14,10},{16,20},{18,... | collective-permute-start | bytes 743432 | tf_op jit(solution)/shard_map/ppermute | solution.py:19
  53.3 10.0 %collective-permute-start.15 = (bf16[88,1408]{1,0:T(8,128)(2,1)S(1)}, bf16[88,1408]{1,0:T(8,128)(2,1)S(1)}, u32[]{:S(2)}, u32[]{:S(2)}) collective-permute-start(bf16[88,1408]{1,0:T(8,128)(2,1)S(1)} %collective-permute-done.3.refs_8_), channel_id=1, source_target_pairs={{0,8},{2,10},{4,12},{6,14},{8,0},{10,2},{12,4},{14,6},{16,24},{18,... | collective-permute-start | bytes 743432 | tf_op jit(solution)/shard_map/ppermute | solution.py:19
  56.5 8.5 %collective-permute-start.18 = (bf16[88,1408]{1,0:T(8,128)(2,1)S(1)}, bf16[88,1408]{1,0:T(8,128)(2,1)S(1)}, u32[]{:S(2)}, u32[]{:S(2)}) collective-permute-start(bf16[88,1408]{1,0:T(8,128)(2,1)S(1)} %collective-permute-done.9.refs_9_), channel_id=1, source_target_pairs={{0,8},{2,10},{4,12},{6,14},{8,0},{10,2},{12,4},{14,6},{16,24},{18,... | collective-permute-start | bytes 743432 | tf_op jit(solution)/shard_map/ppermute | solution.py:19
  56.5 10.2 %collective-permute-start.20 = (bf16[88,1408]{1,0:T(8,128)(2,1)S(1)}, bf16[88,1408]{1,0:T(8,128)(2,1)S(1)}, u32[]{:S(2)}, u32[]{:S(2)}) collective-permute-start(bf16[88,1408]{1,0:T(8,128)(2,1)S(1)} %collective-permute-done.17.refs_14_), channel_id=1, source_target_pairs={{0,4},{2,6},{4,0},{6,2},{8,12},{10,14},{12,8},{14,10},{16,20},{18,... | collective-permute-start | bytes 743432 | tf_op jit(solution)/shard_map/ppermute | solution.py:19
  71.5 2.4 %collective-permute-start.23 = (f32[4,64,704]{2,1,0:T(8,128)S(1)}, f32[4,64,704]{2,1,0:T(8,128)S(1)}, u32[]{:S(2)}, u32[]{:S(2)}) collective-permute-start(f32[4,64,704]{2,1,0:T(8,128)S(1)} %bitcast.49), channel_id=1, source_target_pairs={{0,1},{1,0},{2,3},{3,2},{4,5},{5,4},{6,7},{7,6},{8,9},{9,8},{10,11... | collective-permute-start | bytes 2162696 | tf_op jit(solution)/shard_map/ppermute | solution.py:18
  73.0 2.5 %collective-permute-start.22 = (f32[4,64,704]{2,1,0:T(8,128)S(1)}, f32[4,64,704]{2,1,0:T(8,128)S(1)}, u32[]{:S(2)}, u32[]{:S(2)}) collective-permute-start(f32[4,64,704]{2,1,0:T(8,128)S(1)} %bitcast.50), channel_id=1, source_target_pairs={{0,1},{1,0},{2,3},{3,2},{4,5},{5,4},{6,7},{7,6},{8,9},{9,8},{10,11... | collective-permute-start | bytes 2162696 | tf_op jit(solution)/shard_map/ppermute | solution.py:18
  73.6 12.0 %collective-permute-start.26 = (f32[4,64,704]{2,1,0:T(8,128)S(1)}, f32[4,64,704]{2,1,0:T(8,128)S(1)}, u32[]{:S(2)}, u32[]{:S(2)}) collective-permute-start(f32[4,64,704]{2,1,0:T(8,128)S(1)} %bitcast.48), channel_id=1, source_target_pairs={{0,1},{1,0},{2,3},{3,2},{4,5},{5,4},{6,7},{7,6},{8,9},{9,8},{10,11... | collective-permute-start | bytes 2162696 | tf_op jit(solution)/shard_map/ppermute | solution.py:18
  73.9 11.3 %collective-permute-start.24 = (bf16[4,64,704]{2,1,0:T(8,128)(2,1)S(1)}, bf16[4,64,704]{2,1,0:T(8,128)(2,1)S(1)}, u32[]{:S(2)}, u32[]{:S(2)}) collective-permute-start(bf16[4,64,704]{2,1,0:T(8,128)(2,1)S(1)} %bitcast.42), channel_id=1, source_target_pairs={{0,2},{2,0},{4,6},{6,4},{8,10},{10,8},{12,14},{14,12},{16,18},{18,... | collective-permute-start | bytes 1081352 | tf_op jit(solution)/shard_map/ppermute | solution.py:18
  74.4 18.4 %collective-permute-start.21 = (f32[4,64,704]{2,1,0:T(8,128)S(1)}, f32[4,64,704]{2,1,0:T(8,128)S(1)}, u32[]{:S(2)}, u32[]{:S(2)}) collective-permute-start(f32[4,64,704]{2,1,0:T(8,128)S(1)} %bitcast.47), channel_id=1, source_target_pairs={{0,1},{1,0},{2,3},{3,2},{4,5},{5,4},{6,7},{7,6},{8,9},{9,8},{10,11... | collective-permute-start | bytes 2162696 | tf_op jit(solution)/shard_map/ppermute | solution.py:18
  85.2 10.4 %collective-permute-start.25 = (bf16[4,64,704]{2,1,0:T(8,128)(2,1)S(1)}, bf16[4,64,704]{2,1,0:T(8,128)(2,1)S(1)}, u32[]{:S(2)}, u32[]{:S(2)}) collective-permute-start(bf16[4,64,704]{2,1,0:T(8,128)(2,1)S(1)} %bitcast.40), channel_id=1, source_target_pairs={{0,2},{2,0},{4,6},{6,4},{8,10},{10,8},{12,14},{14,12},{16,18},{18,... | collective-permute-start | bytes 1081352 | tf_op jit(solution)/shard_map/ppermute | solution.py:18
  86.0 1.4 %collective-permute-start.27 = (f32[256,2]{1,0:T(8,128)S(1)}, f32[256,2]{1,0:T(8,128)S(1)}, u32[]{:S(2)}, u32[]{:S(2)}) collective-permute-start(f32[256,2]{1,0:T(8,128)S(1)} %get-tuple-element.82.mine), channel_id=1, source_target_pairs={{0,1},{1,0},{2,3},{3,2},{4,5},{5,4},{6,7},{7,6},{8,9},{9,8},{10,11... | collective-permute-start | bytes 6152 | tf_op jit(solution)/shard_map/ppermute | solution.py:19
  97.3 4.4 %collective-permute-start.29 = (f32[2,8,704]{2,1,0:T(8,128)S(1)}, f32[2,8,704]{2,1,0:T(8,128)S(1)}, u32[]{:S(2)}, u32[]{:S(2)}) collective-permute-start(f32[2,8,704]{2,1,0:T(8,128)S(1)} %get-tuple-element.92), channel_id=1, source_target_pairs={{0,2},{2,0},{4,6},{6,4},{8,10},{10,8},{12,14},{14,12},{16,18},{18,... | collective-permute-start | bytes 135176 | tf_op jit(solution)/shard_map/ppermute | solution.py:19
  97.7 4.3 %collective-permute-start.30 = (f32[2,8,704]{2,1,0:T(8,128)S(1)}, f32[2,8,704]{2,1,0:T(8,128)S(1)}, u32[]{:S(2)}, u32[]{:S(2)}) collective-permute-start(f32[2,8,704]{2,1,0:T(8,128)S(1)} %get-tuple-element.93), channel_id=1, source_target_pairs={{0,4},{2,6},{4,0},{6,2},{8,12},{10,14},{12,8},{14,10},{16,20},{18,... | collective-permute-start | bytes 135176 | tf_op jit(solution)/shard_map/ppermute | solution.py:19
  99.4 5.6 %collective-permute-start.31 = (f32[2,8,704]{2,1,0:T(8,128)S(1)}, f32[2,8,704]{2,1,0:T(8,128)S(1)}, u32[]{:S(2)}, u32[]{:S(2)}) collective-permute-start(f32[2,8,704]{2,1,0:T(8,128)S(1)} %get-tuple-element.94), channel_id=1, source_target_pairs={{0,6},{2,4},{4,2},{6,0},{8,14},{10,12},{12,10},{14,8},{16,22},{18,... | collective-permute-start | bytes 135176 | tf_op jit(solution)/shard_map/ppermute | solution.py:19
  100.8 10.3 %collective-permute-start.35 = (bf16[3,64,704]{2,1,0:T(8,128)(2,1)S(1)}, bf16[3,64,704]{2,1,0:T(8,128)(2,1)S(1)}, u32[]{:S(2)}, u32[]{:S(2)}) collective-permute-start(bf16[3,64,704]{2,1,0:T(8,128)(2,1)S(1)} %get-tuple-element.96), channel_id=1, source_target_pairs={{0,2},{2,0},{4,6},{6,4},{8,10},{10,8},{12,14},{14,12},{16,18},{18,... | collective-permute-start | bytes 811016 | tf_op jit(solution)/shard_map/ppermute | solution.py:19
  105.0 8.3 %collective-permute-start.34 = (f32[2,8,704]{2,1,0:T(8,128)S(1)}, f32[2,8,704]{2,1,0:T(8,128)S(1)}, u32[]{:S(2)}, u32[]{:S(2)}) collective-permute-start(f32[2,8,704]{2,1,0:T(8,128)S(1)} %add_add_fusion.1), channel_id=1, source_target_pairs={{0,8},{2,10},{4,12},{6,14},{8,0},{10,2},{12,4},{14,6},{16,24},{18,... | collective-permute-start | bytes 135176 | tf_op jit(solution)/shard_map/ppermute | solution.py:19
  105.3 8.1 %collective-permute-start.33 = (f32[2,8,704]{2,1,0:T(8,128)S(1)}, f32[2,8,704]{2,1,0:T(8,128)S(1)}, u32[]{:S(2)}, u32[]{:S(2)}) collective-permute-start(f32[2,8,704]{2,1,0:T(8,128)S(1)} %add_add_fusion.1), channel_id=1, source_target_pairs={{0,16},{2,18},{4,20},{6,22},{8,24},{10,26},{12,28},{14,30},{16,0},... | collective-permute-start | bytes 135176 | tf_op jit(solution)/shard_map/ppermute | solution.py:19
  108.8 5.9 %collective-permute-start.32 = (f32[2,8,704]{2,1,0:T(8,128)S(1)}, f32[2,8,704]{2,1,0:T(8,128)S(1)}, u32[]{:S(2)}, u32[]{:S(2)}) collective-permute-start(f32[2,8,704]{2,1,0:T(8,128)S(1)} %add_add_fusion.1), channel_id=1, source_target_pairs={{0,24},{2,26},{4,28},{6,30},{8,16},{10,18},{12,20},{14,22},{16,8},... | collective-permute-start | bytes 135176 | tf_op jit(solution)/shard_map/ppermute | solution.py:19
  109.4 8.9 %collective-permute-start.28 = (bf16[3,64,704]{2,1,0:T(8,128)(2,1)S(1)}, bf16[3,64,704]{2,1,0:T(8,128)(2,1)S(1)}, u32[]{:S(2)}, u32[]{:S(2)}) collective-permute-start(bf16[3,64,704]{2,1,0:T(8,128)(2,1)S(1)} %get-tuple-element.90), channel_id=1, source_target_pairs={{0,2},{2,0},{4,6},{6,4},{8,10},{10,8},{12,14},{14,12},{16,18},{18,... | collective-permute-start | bytes 811016 | tf_op jit(solution)/shard_map/ppermute | solution.py:19
  111.1 7.2 %collective-permute-start.36 = (bf16[3,64,704]{2,1,0:T(8,128)(2,1)S(1)}, bf16[3,64,704]{2,1,0:T(8,128)(2,1)S(1)}, u32[]{:S(2)}, u32[]{:S(2)}) collective-permute-start(bf16[3,64,704]{2,1,0:T(8,128)(2,1)S(1)} %collective-permute-done.35), channel_id=1, source_target_pairs={{0,4},{4,8},{8,12},{12,16},{16,20},{20,24},{24,28},{6,2},{10,6},{1... | collective-permute-start | bytes 811016 | tf_op jit(solution)/shard_map/ppermute | solution.py:49
  114.7 7.7 %collective-permute-start.39 = (f32[2,8,704]{2,1,0:T(8,128)S(1)}, f32[2,8,704]{2,1,0:T(8,128)S(1)}, u32[]{:S(2)}, u32[]{:S(2)}) collective-permute-start(f32[2,8,704]{2,1,0:T(8,128)S(1)} %add_add_fusion.c0), channel_id=1, source_target_pairs={{0,6},{2,4},{4,2},{6,0},{8,14},{10,12},{12,10},{14,8},{16,22},{18,... | collective-permute-start | bytes 135176 | tf_op jit(solution)/shard_map/ppermute | solution.py:19
  116.3 6.1 %collective-permute-start.38 = (f32[2,8,704]{2,1,0:T(8,128)S(1)}, f32[2,8,704]{2,1,0:T(8,128)S(1)}, u32[]{:S(2)}, u32[]{:S(2)}) collective-permute-start(f32[2,8,704]{2,1,0:T(8,128)S(1)} %add_add_fusion.c0), channel_id=1, source_target_pairs={{0,4},{2,6},{4,0},{6,2},{8,12},{10,14},{12,8},{14,10},{16,20},{18,... | collective-permute-start | bytes 135176 | tf_op jit(solution)/shard_map/ppermute | solution.py:19
  117.1 5.3 %collective-permute-start.37 = (f32[2,8,704]{2,1,0:T(8,128)S(1)}, f32[2,8,704]{2,1,0:T(8,128)S(1)}, u32[]{:S(2)}, u32[]{:S(2)}) collective-permute-start(f32[2,8,704]{2,1,0:T(8,128)S(1)} %add_add_fusion.c0), channel_id=1, source_target_pairs={{0,2},{2,0},{4,6},{6,4},{8,10},{10,8},{12,14},{14,12},{16,18},{18,... | collective-permute-start | bytes 135176 | tf_op jit(solution)/shard_map/ppermute | solution.py:19
where the time goes:
time: 124 us
  starting transfers between devices  51.1 us (41%)
  waiting for transfers between devices  35.3 us (28%)
  Pallas kernels  23 us (19%)
  blocking collectives  9.42 us (8%)
  local copies, waits for them, and re-layouts  2.48 us (2%)
  other arithmetic  1.49 us (1%)
    ppermute x30, starting transfers between devices, sent(): return lax.ppermute(value, axis, pairs)  41.4 us
    pallas_call x12, Pallas kernels, call(): pl.pallas_call(body, out_shape=tuple(outs), in_specs=[SMEM] * len(scalars...  23 us
    ppermute x30, waiting for transfers between devices, sent(): return lax.ppermute(value, axis, pairs)  21.4 us
    ppermute x8, waiting for transfers between devices, sent(): lax.ppermute(value.reshape(4, -1, 704), axis, pairs).reshape(value.shape)  13.9 us
    all_gather x4, blocking collectives, both(): lax.all_gather(value.reshape(4, rows // 4, width), 'col', axis=0, tiled=F...  9.42 us
    ppermute x8, starting transfers between devices, sent(): lax.ppermute(value.reshape(4, -1, 704), axis, pairs).reshape(value.shape)  5.11 us
    ppermute x2, starting transfers between devices, neighbours(): return (exchanged(direct, 1), lax.ppermute(through, 'row', pairs))  4.6 us
  transfers between devices with their start and end apart: 40, of which 15 were waited for; matrix products, arithmetic and copies ran while one was open for 2% of the time, Pallas kernels for 12%

commit v1 on v0

--- a/solution.py
+++ b/solution.py
@@ -182,7 +182,7 @@
     core = place[1]
     main, tail = split_of(width)
     for index, block in enumerate(blocks):
-        mask = 2 * (index % 8) + index // 8
+        mask = (0, 1, 4, 5, 8, 9, 12, 13)[index % 8] + 2 * (index // 8)
         source = jnp.bitwise_xor(place[0], mask)
         side = jnp.bitwise_xor(jnp.right_shift(source, 3), place[1])
         start = side * half + jnp.bitwise_and(source, 7) * rows
@@ -309,19 +309,11 @@
         handed[...] = narrow[rows - 3 :]
 
 
-def result_body(place, image, mine, other, across, cot, params, *refs):
+def result_body(image, mine, other, across, cot, params, c0, c1, c2, c3, result, total):
     branch = mine[...] + other[...] + across[...].astype(jnp.float32)
-    result = refs[4]
     result[...] = (image[...].astype(jnp.float32) + params[2:3, :] * branch).astype(jnp.bfloat16)
-    last = jnp.sum(cot[...].astype(jnp.float32) * branch, axis=0, keepdims=True)
-    mine_is = jnp.bitwise_and(place[0], 3)
-    for mask in range(4):
-        chunk, out = refs[mask], refs[5 + mask]
-        out[...] = chunk[...]
-
-        @pl.when(jnp.bitwise_xor(mine_is, mask) == 1)
-        def _():
-            out[0, 7:8, :] = last
+    total[...] = c0[...] + c1[...] + c2[...] + c3[...]
+    total[0, 7:8, :] = jnp.sum(cot[...].astype(jnp.float32) * branch, axis=0, keepdims=True)
 
 
 def terms_body(
@@ -346,8 +338,8 @@
                 sums[tap, col : col + 1, lanes] = jnp.sum(total[tap], axis=0, keepdims=True)
 
     each_lanes(width, part)
-    sums[0, 7:8, :] = jnp.sum(norm_grad[...] * normal[...], axis=0, keepdims=True)
-    sums[1, 7:8, :] = jnp.sum(norm_grad[...], axis=0, keepdims=True)
+    sums[7, 0:1, :] = jnp.sum(norm_grad[...] * normal[...], axis=0, keepdims=True)
+    sums[7, 1:2, :] = jnp.sum(norm_grad[...], axis=0, keepdims=True)
     for mask, chunk in enumerate((c0, c1, c2, c3)):
         chunk[...] = sums[pl.ds(2 * jnp.bitwise_xor(jnp.bitwise_and(place[0], 3), mask), 2)]
 
@@ -371,8 +363,8 @@
         index = 2 * jnp.bitwise_xor(jnp.bitwise_and(place[0], 3), mask)
         sums[pl.ds(index, 2)] = chunk[...] * factor
     kernel_sum[...] = sums[0:7, 0:7, :]
-    for row in range(3):
-        param_sum[row : row + 1, :] = sums[row, 7:8, :]
+    param_sum[0:2, :] = sums[7, 0:2, :]
+    param_sum[2:3, :] = sums[0, 7:8, :] + sums[2, 7:8, :] + sums[4, 7:8, :] + sums[6, 7:8, :]
 
 
 def paired(image, kernel, ln_gain, ln_bias, layer_scale, w_in, w_out, cotangent):
@@ -387,41 +379,43 @@
 
     w_in = after(w_in, direct, handed)
     first, second = packed(w_in, w_out.T, 0), packed(w_in, w_out.T, 1)
-    near = {0: jnp.where(even, first, second)}
-    far = {0: exchanged(jnp.where(even, second, first), 1)}
+    upper = (row & 2) == 0
+    near = {0: jnp.where(upper, first, second)}
+    far = {0: exchanged(jnp.where(upper, second, first), 2)}
     near[8] = exchanged(near[0], 8)
-    near[2] = exchanged(near[0], 2)
-    near[4] = exchanged(after(near[0], near[2]), 4)
+    near[1] = exchanged(near[0], 1)
+    near[4] = exchanged(after(near[0], near[1]), 4)
     shape = pltpu.VMEM((slab_rows + 6, grid_cols, width_part), jnp.float32)
     wide = pltpu.VMEM((7, slab_rows, grid_cols + 16, 128), jnp.float32)
     macs = 98 * tokens * width_part
     conved, stats = call(
         conv_body,
         (f32(tokens, width_part), f32(tokens, 2)),
-        (next_rows, image, after(beyond_rows, far[0], near[2]), kernel),
+        (next_rows, image, beyond_rows, kernel),
         "conv",
         scalars=(place,),
         scratch=[shape, wide],
         flops=macs * 1000,
     )
-    far[2] = exchanged(after(far[0], near[2]), 2)
+    far[1] = exchanged(after(far[0], near[1]), 1)
     far[8] = exchanged(after(far[0], near[8]), 8)
-    near[10] = exchanged(after(near[8], next_rows), 2)
-    near[6] = exchanged(after(near[4], far[2]), 2)
+    near[9] = exchanged(after(near[8], next_rows), 1)
+    near[5] = exchanged(after(near[4], far[1]), 1)
     near[12] = exchanged(after(near[8], near[4]), 4)
-    far[10] = exchanged(after(far[8], near[6]), 2)
+    far[9] = exchanged(after(far[8], near[5]), 1)
     far[12] = exchanged(far[8], 4)
-    near[14] = exchanged(after(near[12], near[10]), 2)
+    near[13] = exchanged(after(near[12], near[9]), 1)
     far[4] = exchanged(after(far[0], near[12]), 4)
-    far[14] = exchanged(after(far[12], far[10]), 2)
-    far[6] = exchanged(after(far[2], far[12]), 4)
-    weights = [near[m] for m in range(0, 16, 2)] + [far[m] for m in range(0, 16, 2)]
+    far[13] = exchanged(after(far[12], far[9]), 1)
+    far[5] = exchanged(after(far[1], far[12]), 4)
+    masks = (0, 1, 4, 5, 8, 9, 12, 13)
+    weights = [near[m] for m in masks] + [far[m] for m in masks]
 
     params = jnp.stack([ln_gain, ln_bias, layer_scale]).reshape(3, 2, width_part)
     params = lax.dynamic_index_in_dim(params, column, 1, False)
     flat_cot = cotangent.reshape(tokens, width_part)
     scaled = (flat_cot.astype(jnp.float32) * params[2]).astype(jnp.bfloat16)
-    scaled_far = exchanged(after(scaled, next_rows), 1)
+    scaled_far = exchanged(after(scaled, next_rows), 2)
     scaled_all = (both(scaled), both(scaled_far))
 
     normal, inverse, normed = call(
@@ -431,14 +425,14 @@
         "norm",
         flops=6 * tokens * width_part,
     )
-    normed_far = exchanged(after(normed, scaled_far), 1)
+    normed_far = exchanged(after(normed, scaled_far), 2)
     normed_all = (both(normed), both(normed_far))
 
     outs = mlp(place, normed_all, scaled_all, weights)
     grad_there_far, grad_there, grad_far, grad_own = outs[:4]
     act_there_far, act_there, act_far, act_own = outs[4:]
-    grad_across = exchanged(joined(grad_far, siblings(grad_there_far)), 1)
-    act_across = exchanged(after(joined(act_far, siblings(act_there_far)), grad_across), 1)
+    grad_across = exchanged(joined(grad_far, siblings(grad_there_far)), 2)
+    act_across = exchanged(after(joined(act_far, siblings(act_there_far)), grad_across), 2)
 
     norm_grad, back_stats = call(
         grad_body,
@@ -473,9 +467,9 @@
         ],
         flops=macs,
     )
-    result, *chunks = call(
+    result, total = call(
         result_body,
-        (bf16(tokens, width_part), *(f32(2, 8, width_part),) * 4),
+        (bf16(tokens, width_part), f32(2, 8, width_part)),
         (
             image.reshape(tokens, width_part),
             act_own,
@@ -483,13 +477,14 @@
             act_across,
             flat_cot,
             params,
-            *chunks,
+            chunks[0],
+            exchanged(chunks[1], 1),
+            exchanged(chunks[2], 2),
+            exchanged(chunks[3], 3),
         ),
         "result",
-        scalars=(place,),
         flops=4 * tokens * width_part,
     )
-    total = chunks[0] + exchanged(chunks[1], 1) + exchanged(chunks[2], 2) + exchanged(chunks[3], 3)
     total = total + exchanged(total, 12) + exchanged(total, 8) + exchanged(total, 4)
     totals = (total, exchanged(total, 3), exchanged(total, 2), exchanged(total, 1))
     totals = (totals[0], totals[3], totals[2], totals[1])

time: 124 us -> 124 us (level)
  starting transfers between devices: 51.1 us -> 56.2 us
  waiting for transfers between devices: 35.3 us -> 30.8 us
    ppermute x30, starting transfers between devices: 41.4 us -> 44.8 us  [sent(): return lax.ppermute(value, axis, pairs)]
    ppermute x8, waiting for transfers between devices: 13.9 us -> 10.6 us  [sent(): lax.ppermute(value.reshape(4, -1, 704), axis, pairs).reshape(value.shape)]
    ppermute x30, waiting for transfers between devices: 21.4 us -> 18.7 us  [sent(): return lax.ppermute(value, axis, pairs)]
    ppermute x2, waiting for transfers between devices: 0.01 us -> 1.44 us  [neighbours(): return (exchanged(direct, 1), lax.ppermute(through, 'row', pairs))]
  transfers between devices with their start and end apart: 40 -> 40, of which waited for: 15 -> 14; matrix products, arithmetic and copies ran while one was open for 2% -> 2% of each run, Pallas kernels for 12% -> 13%
where the time goes in v1:
time: 124 us
  starting transfers between devices  56.2 us (45%)
  waiting for transfers between devices  30.8 us (25%)
  Pallas kernels  22.5 us (18%)
  blocking collectives  9.42 us (8%)
  local copies, waits for them, and re-layouts  2.48 us (2%)
  other arithmetic  1.48 us (1%)
    ppermute x30, starting transfers between devices, sent(): return lax.ppermute(value, axis, pairs)  44.8 us
    pallas_call x12, Pallas kernels, call(): pl.pallas_call(body, out_shape=tuple(outs), in_specs=[SMEM] * len(scalars...  22.5 us
    ppermute x30, waiting for transfers between devices, sent(): return lax.ppermute(value, axis, pairs)  18.7 us
    ppermute x8, waiting for transfers between devices, sent(): lax.ppermute(value.reshape(4, -1, 704), axis, pairs).reshape(value.shape)  10.6 us
    all_gather x4, blocking collectives, both(): lax.all_gather(value.reshape(4, rows // 4, width), 'col', axis=0, tiled=F...  9.42 us
    ppermute x2, starting transfers between devices, neighbours(): return (exchanged(direct, 1), lax.ppermute(through, 'row', pairs))  5.7 us
    ppermute x8, starting transfers between devices, sent(): lax.ppermute(value.reshape(4, -1, 704), axis, pairs).reshape(value.shape)  5.69 us
  transfers between devices with their start and end apart: 40, of which 14 were waited for; matrix products, arithmetic and copies ran while one was open for 2% of the time, Pallas kernels for 13%

profile of v1, /device:TPU:0, one launch (start us, length us, event | category | flops | bytes accessed | tf_op | source)
XLA Modules:
  0.0 123.7 jit_solution(13558111670116907856)
XLA Ops:
  0.7 1.2 broadcast_select_fusion
  1.9 3.0 %collective-permute-start.1 = (bf16[3,64,704]{2,1,0:T(8,128)(2,1)S(1)}, bf16[3,64,704]{2,1,0:T(8,128)(2,1)S(1)}, u32[]{:S(2)}, u32[]{:S(2)}) collective-permute-start(bf16[3,64,704]{2,1,0:T(8,128)(2,1)S(1)} %get-tuple-element.94), channel_id=1, source_target_pairs={{0,2},{2,0},{4,6},{6,4},{8,10},{10,8},{12,14},{14,12},{16,18},{18,... | collective-permute-start | bytes 811016 | tf_op jit(solution)/shard_map/ppermute | solution.py:19
  4.9 0.9 fusion.2
  5.8 1.1 fusion.4
  7.2 1.6 %collective-permute-start.8 = (bf16[88,1408]{1,0:T(8,128)(2,1)S(1)}, bf16[88,1408]{1,0:T(8,128)(2,1)S(1)}, u32[]{:S(2)}, u32[]{:S(2)}) collective-permute-start(bf16[88,1408]{1,0:T(8,128)(2,1)S(1)} %get-tuple-element.92), channel_id=1, source_target_pairs={{0,4},{2,6},{4,0},{6,2},{8,12},{10,14},{12,8},{14,10},{16,20},{18,... | collective-permute-start | bytes 743432 | tf_op jit(solution)/shard_map/ppermute | solution.py:19
  8.7 0.5 collective-permute-start.6
  9.3 1.5 %collective-permute-start = (bf16[3,64,704]{2,1,0:T(8,128)(2,1)S(1)}, bf16[3,64,704]{2,1,0:T(8,128)(2,1)S(1)}, u32[]{:S(2)}, u32[]{:S(2)}) collective-permute-start(bf16[3,64,704]{2,1,0:T(8,128)(2,1)S(1)} %get-tuple-element.95), channel_id=1, source_target_pairs={{0,2},{2,0},{4,6},{6,4},{8,10},{10,8},{12,14},{14,12},{16,18},{18,... | collective-permute-start | bytes 811016 | tf_op jit(solution)/shard_map/ppermute | solution.py:19
  10.8 2.6 %collective-permute-start.11 = (bf16[88,1408]{1,0:T(8,128)(2,1)S(1)}, bf16[88,1408]{1,0:T(8,128)(2,1)S(1)}, u32[]{:S(2)}, u32[]{:S(2)}) collective-permute-start(bf16[88,1408]{1,0:T(8,128)(2,1)S(1)} %get-tuple-element.53.refs_0_), channel_id=1, source_target_pairs={{0,16},{2,18},{4,20},{6,22},{8,24},{10,26},{12,28},{14,30},{16,0},... | collective-permute-start | bytes 743432 | tf_op jit(solution)/shard_map/ppermute | solution.py:19
  13.6 1.0 collective-permute-done.8.refs_8_
  14.7 3.3 %collective-permute-done.6.refs_1_ = bf16[88,1408]{1,0:T(8,128)(2,1)S(1)} collective-permute-done((bf16[88,1408]{1,0:T(8,128)(2,1)S(1)}, bf16[88,1408]{1,0:T(8,128)(2,1)S(1)}, u32[]{:S(2)}, u32[]{:S(2)}) %collective-permute-start.6) | collective-permute-done | bytes 247840 | tf_op jit(solution)/shard_map/ppermute | solution.py:19
  18.0 2.1 %collective-permute-start.7 = (bf16[88,1408]{1,0:T(8,128)(2,1)S(1)}, bf16[88,1408]{1,0:T(8,128)(2,1)S(1)}, u32[]{:S(2)}, u32[]{:S(2)}) collective-permute-start(bf16[88,1408]{1,0:T(8,128)(2,1)S(1)} %get-tuple-element.53.refs_0_), channel_id=1, source_target_pairs={{0,8},{2,10},{4,12},{6,14},{8,0},{10,2},{12,4},{14,6},{16,24},{18,... | collective-permute-start | bytes 743432 | tf_op jit(solution)/shard_map/ppermute | solution.py:19
  20.2 1.5 %collective-permute-start.9 = (bf16[88,1408]{1,0:T(8,128)(2,1)S(1)}, bf16[88,1408]{1,0:T(8,128)(2,1)S(1)}, u32[]{:S(2)}, u32[]{:S(2)}) collective-permute-start(bf16[88,1408]{1,0:T(8,128)(2,1)S(1)} %collective-permute-done.8.refs_8_), channel_id=1, source_target_pairs={{0,2},{2,0},{4,6},{6,4},{8,10},{10,8},{12,14},{14,12},{16,18},{18,... | collective-permute-start | bytes 743432 | tf_op jit(solution)/shard_map/ppermute | solution.py:19
  21.7 3.4 %collective-permute-start.2 = (bf16[3,64,704]{2,1,0:T(8,128)(2,1)S(1)}, bf16[3,64,704]{2,1,0:T(8,128)(2,1)S(1)}, u32[]{:S(2)}, u32[]{:S(2)}) collective-permute-start(bf16[3,64,704]{2,1,0:T(8,128)(2,1)S(1)} %collective-permute-done.1), channel_id=1, source_target_pairs={{0,4},{4,8},{8,12},{12,16},{16,20},{20,24},{24,28},{6,2},{10,6},{1... | collective-permute-start | bytes 811016 | tf_op jit(solution)/shard_map/ppermute | solution.py:49
  25.3 2.6 %collective-permute-start.16 = (bf16[88,1408]{1,0:T(8,128)(2,1)S(1)}, bf16[88,1408]{1,0:T(8,128)(2,1)S(1)}, u32[]{:S(2)}, u32[]{:S(2)}) collective-permute-start(bf16[88,1408]{1,0:T(8,128)(2,1)S(1)} %collective-permute-done.8.refs_8_), channel_id=1, source_target_pairs={{0,16},{2,18},{4,20},{6,22},{8,24},{10,26},{12,28},{14,30},{16,0},... | collective-permute-start | bytes 743432 | tf_op jit(solution)/shard_map/ppermute | solution.py:19
  27.9 2.6 %collective-permute-done.7.refs_2_ = bf16[88,1408]{1,0:T(8,128)(2,1)S(1)} collective-permute-done((bf16[88,1408]{1,0:T(8,128)(2,1)S(1)}, bf16[88,1408]{1,0:T(8,128)(2,1)S(1)}, u32[]{:S(2)}, u32[]{:S(2)}) %collective-permute-start.7) | collective-permute-done | bytes 247840 | tf_op jit(solution)/shard_map/ppermute | solution.py:19
  30.6 1.2 collective-permute-start.10
  31.7 3.6 %conv.1 = (f32[256,704]{1,0:T(8,128)S(1)}, f32[256,2]{1,0:T(8,128)S(1)}) custom-call(s32[2]{0:T(128)S(1)} %pad_add_fusion.place, bf16[3,64,704]{2,1,0:T(8,128)(2,1)S(1)} %collective-permute-done.near, bf16[4,64,704]{2,1,0:T(8,128)(2,1)S(1)} %copy-done.1, bf16[3,64,704]{2,1,0:T(8,128)(2,1)S(1)} %collective-permute-done.2.beyond, f32[7,7,704]{2,1,0:T(8,128)S(1)} %copy-done.2), custom_call_target="tpu_custom_call" | custom-call | flops 17661952000 | bytes 1762048 | tf_op jit(solution)/shard_map/conv/pallas_call | solution.py:54
  35.5 2.7 %collective-permute-start.5 = (bf16[4,64,704]{2,1,0:T(8,128)(2,1)S(1)}, bf16[4,64,704]{2,1,0:T(8,128)(2,1)S(1)}, u32[]{:S(2)}, u32[]{:S(2)}) collective-permute-start(bf16[4,64,704]{2,1,0:T(8,128)(2,1)S(1)} %bitcast.51), channel_id=1, source_target_pairs={{0,4},{2,6},{4,0},{6,2},{8,12},{10,14},{12,8},{14,10},{16,20},{18,... | collective-permute-start | bytes 1081352 | tf_op jit(solution)/shard_map/ppermute | solution.py:18
  38.2 8.3 %collective-permute-start.12 = (bf16[88,1408]{1,0:T(8,128)(2,1)S(1)}, bf16[88,1408]{1,0:T(8,128)(2,1)S(1)}, u32[]{:S(2)}, u32[]{:S(2)}) collective-permute-start(bf16[88,1408]{1,0:T(8,128)(2,1)S(1)} %collective-permute-done.11.refs_4_), channel_id=1, source_target_pairs={{0,2},{2,0},{4,6},{6,4},{8,10},{10,8},{12,14},{14,12},{16,18},{18,... | collective-permute-start | bytes 743432 | tf_op jit(solution)/shard_map/ppermute | solution.py:19
  46.6 2.4 %all-gather.1 = bf16[8,64,704]{2,1,0:T(8,128)(2,1)S(1)} all-gather(bf16[4,64,704]{2,1,0:T(8,128)(2,1)S(1)} %multiply_convert_fusion.1), channel_id=3, replica_groups=mesh['groups'=1,'row'=16,'col'=2] {'col'}, dimensions={0}, use_global_device_ids=true | all-gather | bytes 1081344 | tf_op jit(solution)/shard_map/all_gather | solution.py:33
  49.0 0.3 norm.1
  49.3 1.1 collective-permute-start.4
  50.4 2.4 %all_gather.12 = bf16[2,4,64,704]{3,2,1,0:T(8,128)(2,1)S(1)} all-gather(bf16[1,4,64,704]{3,2,1,0:T(8,128)(2,1)S(1)} %bitcast.38), channel_id=1, replica_groups=mesh['groups'=1,'row'=16,'col'=2] {'col'}, dimensions={0}, use_global_device_ids=true | all-gather | bytes 1081344 | tf_op jit(solution)/shard_map/all_gather | solution.py:33
  52.7 0.5 collective-permute-done.12.refs_5_
  53.2 2.1 %collective-permute-start.14 = (bf16[88,1408]{1,0:T(8,128)(2,1)S(1)}, bf16[88,1408]{1,0:T(8,128)(2,1)S(1)}, u32[]{:S(2)}, u32[]{:S(2)}) collective-permute-start(bf16[88,1408]{1,0:T(8,128)(2,1)S(1)} %collective-permute-done.13.refs_6_), channel_id=1, source_target_pairs={{0,2},{2,0},{4,6},{6,4},{8,10},{10,8},{12,14},{14,12},{16,18},{18,... | collective-permute-start | bytes 743432 | tf_op jit(solution)/shard_map/ppermute | solution.py:19
  55.3 0.4 collective-permute-start.15
  55.7 2.9 %collective-permute-done.19.refs_13_ = bf16[88,1408]{1,0:T(8,128)(2,1)S(1)} collective-permute-done((bf16[88,1408]{1,0:T(8,128)(2,1)S(1)}, bf16[88,1408]{1,0:T(8,128)(2,1)S(1)}, u32[]{:S(2)}, u32[]{:S(2)}) %collective-permute-start.19) | collective-permute-done | bytes 247840 | tf_op jit(solution)/shard_map/ppermute | solution.py:19
  58.6 2.1 %collective-permute-start.20 = (bf16[88,1408]{1,0:T(8,128)(2,1)S(1)}, bf16[88,1408]{1,0:T(8,128)(2,1)S(1)}, u32[]{:S(2)}, u32[]{:S(2)}) collective-permute-start(bf16[88,1408]{1,0:T(8,128)(2,1)S(1)} %collective-permute-done.17.refs_14_), channel_id=1, source_target_pairs={{0,2},{2,0},{4,6},{6,4},{8,10},{10,8},{12,14},{14,12},{16,18},{18,... | collective-permute-start | bytes 743432 | tf_op jit(solution)/shard_map/ppermute | solution.py:19
  60.6 2.4 %all-gather.2 = bf16[8,64,704]{2,1,0:T(8,128)(2,1)S(1)} all-gather(bf16[4,64,704]{2,1,0:T(8,128)(2,1)S(1)} %collective-permute-done.5), channel_id=4, replica_groups=mesh['groups'=1,'row'=16,'col'=2] {'col'}, dimensions={0}, use_global_device_ids=true | all-gather | bytes 1081344 | tf_op jit(solution)/shard_map/all_gather | solution.py:33
  63.0 2.4 %all-gather = bf16[8,64,704]{2,1,0:T(8,128)(2,1)S(1)} all-gather(bf16[4,64,704]{2,1,0:T(8,128)(2,1)S(1)} %collective-permute-done.4), channel_id=2, replica_groups=mesh['groups'=1,'row'=16,'col'=2] {'col'}, dimensions={0}, use_global_device_ids=true | all-gather | bytes 1081344 | tf_op jit(solution)/shard_map/all_gather | solution.py:33
  65.4 1.7 %collective-permute-done.18.refs_11_ = bf16[88,1408]{1,0:T(8,128)(2,1)S(1)} collective-permute-done((bf16[88,1408]{1,0:T(8,128)(2,1)S(1)}, bf16[88,1408]{1,0:T(8,128)(2,1)S(1)}, u32[]{:S(2)}, u32[]{:S(2)}) %collective-permute-start.18) | collective-permute-done | bytes 247840 | tf_op jit(solution)/shard_map/ppermute | solution.py:19
  67.0 1.7 %collective-permute-done.20.refs_15_ = bf16[88,1408]{1,0:T(8,128)(2,1)S(1)} collective-permute-done((bf16[88,1408]{1,0:T(8,128)(2,1)S(1)}, bf16[88,1408]{1,0:T(8,128)(2,1)S(1)}, u32[]{:S(2)}, u32[]{:S(2)}) %collective-permute-start.20) | collective-permute-done | bytes 247840 | tf_op jit(solution)/shard_map/ppermute | solution.py:19
  68.8 4.8 %mlp.1 = (f32[256,704]{1,0:T(8,128)S(1)}, f32[256,704]{1,0:T(8,128)S(1)}, f32[256,704]{1,0:T(8,128)S(1)}, f32[256,704]{1,0:T(8,128)S(1)}, bf16[1408,1408]{1,0:T(8,128)(2,1)S(1)}, /*index=5*/bf16[512,768]{1,0:T(8,128)(2,1)S(1)}) custom-call(s32[2]{0:T(128)S(1)} %pad_add_fusion.place, bf16[2,256,704]{2,1,0:T(8,128)(2,1)S(1)} %bitcast.30, ...), custom_call_target="tpu_custom_call" | custom-call | flops 3045064704 | bytes 14483456 | tf_op jit(solution)/shard_map/mlp/pallas_call | solution.py:54
  73.6 1.4 %branch.1 = (f32[256,704]{1,0:T(8,128)S(1)}, f32[256,704]{1,0:T(8,128)S(1)}, f32[256,704]{1,0:T(8,128)S(1)}, f32[256,704]{1,0:T(8,128)S(1)}) custom-call(bf16[512,768]{1,0:T(8,128)(2,1)S(1)} %get-tuple-element.64.act, bf16[1408,1408]{1,0:T(8,128)(2,1)S(1)} %get-tuple-element.65.whole), custom_call_target="tpu_custom_call" | custom-call | flops 1015021568 | bytes 7634944 | tf_op jit(solution)/shard_map/branch/pallas_call | solution.py:54
  75.0 0.6 collective-permute-start.22
  75.7 0.4 collective-permute-start.21
  76.2 0.4 collective-permute-start.24
  76.6 0.9 collective-permute-done.22
  77.5 0.1 joined.2
  77.7 9.7 %collective-permute-done.24 = bf16[4,64,704]{2,1,0:T(8,128)(2,1)S(1)} collective-permute-done((bf16[4,64,704]{2,1,0:T(8,128)(2,1)S(1)}, bf16[4,64,704]{2,1,0:T(8,128)(2,1)S(1)}, u32[]{:S(2)}, u32[]{:S(2)}) %collective-permute-start.24) | collective-permute-done | bytes 360480 | tf_op jit(solution)/shard_map/ppermute | solution.py:18
  87.4 0.4 collective-permute-start.25
  87.7 0.4 grad.1
  88.2 1.3 %collective-permute-done.27.other = f32[256,2]{1,0:T(8,128)S(1)} collective-permute-done((f32[256,2]{1,0:T(8,128)S(1)}, f32[256,2]{1,0:T(8,128)S(1)}, u32[]{:S(2)}, u32[]{:S(2)}) %collective-permute-start.27) | collective-permute-done | bytes 2080 | tf_op jit(solution)/shard_map/ppermute | solution.py:19
  89.5 0.9 field.1
  90.4 1.8 %collective-permute-start.35 = (bf16[3,64,704]{2,1,0:T(8,128)(2,1)S(1)}, bf16[3,64,704]{2,1,0:T(8,128)(2,1)S(1)}, u32[]{:S(2)}, u32[]{:S(2)}) collective-permute-start(bf16[3,64,704]{2,1,0:T(8,128)(2,1)S(1)} %get-tuple-element.88), channel_id=1, source_target_pairs={{0,2},{2,0},{4,6},{6,4},{8,10},{10,8},{12,14},{14,12},{16,18},{18,... | collective-permute-start | bytes 811016 | tf_op jit(solution)/shard_map/ppermute | solution.py:19
  92.2 4.5 %terms.1 = (f32[2,8,704]{2,1,0:T(8,128)S(1)}, f32[2,8,704]{2,1,0:T(8,128)S(1)}, f32[2,8,704]{2,1,0:T(8,128)S(1)}, f32[2,8,704]{2,1,0:T(8,128)S(1)}) custom-call(s32[2]{0:T(128)S(1)} %pad_add_fusion.place, f32[4,64,704]{2,1,0:T(8,128)S(1)} %get-tuple-element.87.field.middle, bf16[3,64,704]{2,1,0:T(8,128)(2,1)S(1)} %collective-permute-done.near, ...), custom_call_target="tpu_custom_call" | custom-call | flops 17661952 | bytes 3244032 | tf_op jit(solution)/shard_map/terms/pallas_call | solution.py:54
  96.7 0.3 collective-permute-start.28
  97.0 1.7 %collective-permute-start.29 = (f32[2,8,704]{2,1,0:T(8,128)S(1)}, f32[2,8,704]{2,1,0:T(8,128)S(1)}, u32[]{:S(2)}, u32[]{:S(2)}) collective-permute-start(f32[2,8,704]{2,1,0:T(8,128)S(1)} %get-tuple-element.82), channel_id=1, source_target_pairs={{0,4},{2,6},{4,0},{6,2},{8,12},{10,14},{12,8},{14,10},{16,20},{18,... | collective-permute-start | bytes 135176 | tf_op jit(solution)/shard_map/ppermute | solution.py:19
  98.7 1.5 %collective-permute-start.30 = (f32[2,8,704]{2,1,0:T(8,128)S(1)}, f32[2,8,704]{2,1,0:T(8,128)S(1)}, u32[]{:S(2)}, u32[]{:S(2)}) collective-permute-start(f32[2,8,704]{2,1,0:T(8,128)S(1)} %get-tuple-element.83), channel_id=1, source_target_pairs={{0,6},{2,4},{4,2},{6,0},{8,14},{10,12},{12,10},{14,8},{16,22},{18,... | collective-permute-start | bytes 135176 | tf_op jit(solution)/shard_map/ppermute | solution.py:19
  100.2 0.8 collective-permute-done.28.c1
  101.1 2.6 %collective-permute-done.30.c3 = f32[2,8,704]{2,1,0:T(8,128)S(1)} collective-permute-done((f32[2,8,704]{2,1,0:T(8,128)S(1)}, f32[2,8,704]{2,1,0:T(8,128)S(1)}, u32[]{:S(2)}, u32[]{:S(2)}) %collective-permute-start.30) | collective-permute-done | bytes 45088 | tf_op jit(solution)/shard_map/ppermute | solution.py:19
  103.7 1.0 result.1
  104.7 0.2 collective-permute-start.34
  105.0 1.9 %collective-permute-start.33 = (f32[2,8,704]{2,1,0:T(8,128)S(1)}, f32[2,8,704]{2,1,0:T(8,128)S(1)}, u32[]{:S(2)}, u32[]{:S(2)}) collective-permute-start(f32[2,8,704]{2,1,0:T(8,128)S(1)} %get-tuple-element.86), channel_id=1, source_target_pairs={{0,16},{2,18},{4,20},{6,22},{8,24},{10,26},{12,28},{14,30},{16,0},... | collective-permute-start | bytes 135176 | tf_op jit(solution)/shard_map/ppermute | solution.py:19
  106.8 2.3 %collective-permute-start.32 = (f32[2,8,704]{2,1,0:T(8,128)S(1)}, f32[2,8,704]{2,1,0:T(8,128)S(1)}, u32[]{:S(2)}, u32[]{:S(2)}) collective-permute-start(f32[2,8,704]{2,1,0:T(8,128)S(1)} %get-tuple-element.86), channel_id=1, source_target_pairs={{0,24},{2,26},{4,28},{6,30},{8,16},{10,18},{12,20},{14,22},{16,8},... | collective-permute-start | bytes 135176 | tf_op jit(solution)/shard_map/ppermute | solution.py:19
  109.1 1.7 %collective-permute-start.31 = (bf16[3,64,704]{2,1,0:T(8,128)(2,1)S(1)}, bf16[3,64,704]{2,1,0:T(8,128)(2,1)S(1)}, u32[]{:S(2)}, u32[]{:S(2)}) collective-permute-start(bf16[3,64,704]{2,1,0:T(8,128)(2,1)S(1)} %get-tuple-element.85), channel_id=1, source_target_pairs={{0,2},{2,0},{4,6},{6,4},{8,10},{10,8},{12,14},{14,12},{16,18},{18,... | collective-permute-start | bytes 811016 | tf_op jit(solution)/shard_map/ppermute | solution.py:19
  110.9 2.3 %collective-permute-start.36 = (bf16[3,64,704]{2,1,0:T(8,128)(2,1)S(1)}, bf16[3,64,704]{2,1,0:T(8,128)(2,1)S(1)}, u32[]{:S(2)}, u32[]{:S(2)}) collective-permute-start(bf16[3,64,704]{2,1,0:T(8,128)(2,1)S(1)} %collective-permute-done.35), channel_id=1, source_target_pairs={{0,4},{4,8},{8,12},{12,16},{16,20},{20,24},{24,28},{6,2},{10,6},{1... | collective-permute-start | bytes 811016 | tf_op jit(solution)/shard_map/ppermute | solution.py:49
  113.2 1.4 %collective-permute-start.39 = (f32[2,8,704]{2,1,0:T(8,128)S(1)}, f32[2,8,704]{2,1,0:T(8,128)S(1)}, u32[]{:S(2)}, u32[]{:S(2)}) collective-permute-start(f32[2,8,704]{2,1,0:T(8,128)S(1)} %add_add_fusion.c0), channel_id=1, source_target_pairs={{0,6},{2,4},{4,2},{6,0},{8,14},{10,12},{12,10},{14,8},{16,22},{18,... | collective-permute-start | bytes 135176 | tf_op jit(solution)/shard_map/ppermute | solution.py:19
  114.6 1.1 collective-permute-start.38
  115.8 1.0 collective-permute-start.37
  116.8 0.1 collective-permute-done.31.near
  116.9 1.4 %collective-permute-done.36.beyond = bf16[3,64,704]{2,1,0:T(8,128)(2,1)S(1)} collective-permute-done((bf16[3,64,704]{2,1,0:T(8,128)(2,1)S(1)}, bf16[3,64,704]{2,1,0:T(8,128)(2,1)S(1)}, u32[]{:S(2)}, u32[]{:S(2)}) %collective-permute-start.36) | collective-permute-done | bytes 270368 | tf_op jit(solution)/shard_map/ppermute | solution.py:49
  118.3 4.1 %back.1 = bf16[4,64,704]{2,1,0:T(8,128)(2,1)} custom-call(s32[2]{0:T(128)S(1)} %pad_add_fusion.place, bf16[3,64,704]{2,1,0:T(8,128)(2,1)S(1)} %collective-permute-done.31.near, f32[4,64,704]{2,1,0:T(8,128)S(1)} %get-tuple-element.87.field.middle, bf16[3,64,704]{2,1,0:T(8,128)(2,1)S(1)} %collective-permute-done.36.beyond, f32[7,7,704]{2,1,0:T(8,128)S(1)} %copy-done.2, ...), custom_call_target="tpu_custom_call" | custom-call | flops 17661952 | bytes 2120448 | tf_op jit(solution)/shard_map/back/pallas_call | solution.py:54
  122.5 1.2 %final.1 = (f32[7,7,704]{2,1,0:T(8,128)}, f32[3,704]{1,0:T(4,128)}) custom-call(s32[2]{0:T(128)S(1)} %pad_add_fusion.place, f32[2,8,704]{2,1,0:T(8,128)S(1)} %add_add_fusion.c0, f32[2,8,704]{2,1,0:T(8,128)S(1)} %collective-permute-done.37.c1, f32[2,8,704]{2,1,0:T(8,128)S(1)} %collective-permute-done.38.c2, f32[2,8,704]{2,1,0:T(8,128)S(1)} %collective-permute-done.39.c3), custom_call_target="tpu_custom_call" | custom-call | bytes 326656 | tf_op jit(solution)/shard_map/final/pallas_call | solution.py:54
  (59 shorter events, 1.4 us)
Async XLA Ops:
  0.6 31.1 %copy-start.1 = (bf16[4,64,704]{2,1,0:T(8,128)(2,1)S(1)}, bf16[4,64,704]{2,1,0:T(8,128)(2,1)}, u32[]{:S(2)}) copy-start(bf16[4,64,704]{2,1,0:T(8,128)(2,1)} %middle.3) | copy-start | bytes 1081348
  0.6 12.7 %copy-start.3 = (f32[1408]{0:T(1024)S(1)}, f32[1408]{0:T(1024)}, u32[]{:S(2)}) copy-start(f32[1408]{0:T(1024)} %param.10) | copy-start | bytes 16900
  0.7 12.8 %copy-start.4 = (f32[1408]{0:T(1024)S(1)}, f32[1408]{0:T(1024)}, u32[]{:S(2)}) copy-start(f32[1408]{0:T(1024)} %param.11) | copy-start | bytes 16900
  0.7 12.9 %copy-start.5 = (f32[1408]{0:T(1024)S(1)}, f32[1408]{0:T(1024)}, u32[]{:S(2)}) copy-start(f32[1408]{0:T(1024)} %param.12) | copy-start | bytes 16900
  0.7 24.5 %copy-start = (bf16[4,64,704]{2,1,0:T(8,128)(2,1)S(1)}, bf16[4,64,704]{2,1,0:T(8,128)(2,1)}, u32[]{:S(2)}) copy-start(bf16[4,64,704]{2,1,0:T(8,128)(2,1)} %cot.1) | copy-start | bytes 1081348
  0.7 31.1 %copy-start.2 = (f32[7,7,704]{2,1,0:T(8,128)S(1)}, f32[7,7,704]{2,1,0:T(8,128)}, u32[]{:S(2)}) copy-start(f32[7,7,704]{2,1,0:T(8,128)} %kernel.3) | copy-start | bytes 413956
  1.9 19.8 %collective-permute-start.1 = (bf16[3,64,704]{2,1,0:T(8,128)(2,1)S(1)}, bf16[3,64,704]{2,1,0:T(8,128)(2,1)S(1)}, u32[]{:S(2)}, u32[]{:S(2)}) collective-permute-start(bf16[3,64,704]{2,1,0:T(8,128)(2,1)S(1)} %get-tuple-element.94), channel_id=1, source_target_pairs={{0,2},{2,0},{4,6},{6,4},{8,10},{10,8},{12,14},{14,12},{16,18},{18,... | collective-permute-start | bytes 811016 | tf_op jit(solution)/shard_map/ppermute | solution.py:19
  7.2 7.5 %collective-permute-start.8 = (bf16[88,1408]{1,0:T(8,128)(2,1)S(1)}, bf16[88,1408]{1,0:T(8,128)(2,1)S(1)}, u32[]{:S(2)}, u32[]{:S(2)}) collective-permute-start(bf16[88,1408]{1,0:T(8,128)(2,1)S(1)} %get-tuple-element.92), channel_id=1, source_target_pairs={{0,4},{2,6},{4,0},{6,2},{8,12},{10,14},{12,8},{14,10},{16,20},{18,... | collective-permute-start | bytes 743432 | tf_op jit(solution)/shard_map/ppermute | solution.py:19
  8.7 9.3 %collective-permute-start.6 = (bf16[88,1408]{1,0:T(8,128)(2,1)S(1)}, bf16[88,1408]{1,0:T(8,128)(2,1)S(1)}, u32[]{:S(2)}, u32[]{:S(2)}) collective-permute-start(bf16[88,1408]{1,0:T(8,128)(2,1)S(1)} %get-tuple-element.53.refs_0_), channel_id=1, source_target_pairs={{0,2},{2,0},{4,6},{6,4},{8,10},{10,8},{12,14},{14,12},{16,18},{18,... | collective-permute-start | bytes 743432 | tf_op jit(solution)/shard_map/ppermute | solution.py:19
  9.3 22.5 %collective-permute-start = (bf16[3,64,704]{2,1,0:T(8,128)(2,1)S(1)}, bf16[3,64,704]{2,1,0:T(8,128)(2,1)S(1)}, u32[]{:S(2)}, u32[]{:S(2)}) collective-permute-start(bf16[3,64,704]{2,1,0:T(8,128)(2,1)S(1)} %get-tuple-element.95), channel_id=1, source_target_pairs={{0,2},{2,0},{4,6},{6,4},{8,10},{10,8},{12,14},{14,12},{16,18},{18,... | collective-permute-start | bytes 811016 | tf_op jit(solution)/shard_map/ppermute | solution.py:19
  10.8 14.5 %collective-permute-start.11 = (bf16[88,1408]{1,0:T(8,128)(2,1)S(1)}, bf16[88,1408]{1,0:T(8,128)(2,1)S(1)}, u32[]{:S(2)}, u32[]{:S(2)}) collective-permute-start(bf16[88,1408]{1,0:T(8,128)(2,1)S(1)} %get-tuple-element.53.refs_0_), channel_id=1, source_target_pairs={{0,16},{2,18},{4,20},{6,22},{8,24},{10,26},{12,28},{14,30},{16,0},... | collective-permute-start | bytes 743432 | tf_op jit(solution)/shard_map/ppermute | solution.py:19
  18.0 12.5 %collective-permute-start.7 = (bf16[88,1408]{1,0:T(8,128)(2,1)S(1)}, bf16[88,1408]{1,0:T(8,128)(2,1)S(1)}, u32[]{:S(2)}, u32[]{:S(2)}) collective-permute-start(bf16[88,1408]{1,0:T(8,128)(2,1)S(1)} %get-tuple-element.53.refs_0_), channel_id=1, source_target_pairs={{0,8},{2,10},{4,12},{6,14},{8,0},{10,2},{12,4},{14,6},{16,24},{18,... | collective-permute-start | bytes 743432 | tf_op jit(solution)/shard_map/ppermute | solution.py:19
  20.2 10.4 %collective-permute-start.9 = (bf16[88,1408]{1,0:T(8,128)(2,1)S(1)}, bf16[88,1408]{1,0:T(8,128)(2,1)S(1)}, u32[]{:S(2)}, u32[]{:S(2)}) collective-permute-start(bf16[88,1408]{1,0:T(8,128)(2,1)S(1)} %collective-permute-done.8.refs_8_), channel_id=1, source_target_pairs={{0,2},{2,0},{4,6},{6,4},{8,10},{10,8},{12,14},{14,12},{16,18},{18,... | collective-permute-start | bytes 743432 | tf_op jit(solution)/shard_map/ppermute | solution.py:19
  21.7 10.1 %collective-permute-start.2 = (bf16[3,64,704]{2,1,0:T(8,128)(2,1)S(1)}, bf16[3,64,704]{2,1,0:T(8,128)(2,1)S(1)}, u32[]{:S(2)}, u32[]{:S(2)}) collective-permute-start(bf16[3,64,704]{2,1,0:T(8,128)(2,1)S(1)} %collective-permute-done.1), channel_id=1, source_target_pairs={{0,4},{4,8},{8,12},{12,16},{16,20},{20,24},{24,28},{6,2},{10,6},{1... | collective-permute-start | bytes 811016 | tf_op jit(solution)/shard_map/ppermute | solution.py:49
  25.3 12.9 %collective-permute-start.16 = (bf16[88,1408]{1,0:T(8,128)(2,1)S(1)}, bf16[88,1408]{1,0:T(8,128)(2,1)S(1)}, u32[]{:S(2)}, u32[]{:S(2)}) collective-permute-start(bf16[88,1408]{1,0:T(8,128)(2,1)S(1)} %collective-permute-done.8.refs_8_), channel_id=1, source_target_pairs={{0,16},{2,18},{4,20},{6,22},{8,24},{10,26},{12,28},{14,30},{16,0},... | collective-permute-start | bytes 743432 | tf_op jit(solution)/shard_map/ppermute | solution.py:19
  30.6 18.7 %collective-permute-start.13 = (bf16[88,1408]{1,0:T(8,128)(2,1)S(1)}, bf16[88,1408]{1,0:T(8,128)(2,1)S(1)}, u32[]{:S(2)}, u32[]{:S(2)}) collective-permute-start(bf16[88,1408]{1,0:T(8,128)(2,1)S(1)} %collective-permute-done.11.refs_4_), channel_id=1, source_target_pairs={{0,8},{2,10},{4,12},{6,14},{8,0},{10,2},{12,4},{14,6},{16,24},{18,... | collective-permute-start | bytes 743432 | tf_op jit(solution)/shard_map/ppermute | solution.py:19
  30.6 15.9 %collective-permute-start.10 = (bf16[88,1408]{1,0:T(8,128)(2,1)S(1)}, bf16[88,1408]{1,0:T(8,128)(2,1)S(1)}, u32[]{:S(2)}, u32[]{:S(2)}) collective-permute-start(bf16[88,1408]{1,0:T(8,128)(2,1)S(1)} %collective-permute-done.7.refs_2_), channel_id=1, source_target_pairs={{0,2},{2,0},{4,6},{6,4},{8,10},{10,8},{12,14},{14,12},{16,18},{18,... | collective-permute-start | bytes 743432 | tf_op jit(solution)/shard_map/ppermute | solution.py:19
  35.4 11.1 %collective-permute-start.3 = (f32[256,2]{1,0:T(8,128)S(1)}, f32[256,2]{1,0:T(8,128)S(1)}, u32[]{:S(2)}, u32[]{:S(2)}) collective-permute-start(f32[256,2]{1,0:T(8,128)S(1)} %get-tuple-element.49.mine), channel_id=1, source_target_pairs={{0,1},{1,0},{2,3},{3,2},{4,5},{5,4},{6,7},{7,6},{8,9},{9,8},{10,11... | collective-permute-start | bytes 6152 | tf_op jit(solution)/shard_map/ppermute | solution.py:19
  35.5 23.0 %collective-permute-start.5 = (bf16[4,64,704]{2,1,0:T(8,128)(2,1)S(1)}, bf16[4,64,704]{2,1,0:T(8,128)(2,1)S(1)}, u32[]{:S(2)}, u32[]{:S(2)}) collective-permute-start(bf16[4,64,704]{2,1,0:T(8,128)(2,1)S(1)} %bitcast.51), channel_id=1, source_target_pairs={{0,4},{2,6},{4,0},{6,2},{8,12},{10,14},{12,8},{14,10},{16,20},{18,... | collective-permute-start | bytes 1081352 | tf_op jit(solution)/shard_map/ppermute | solution.py:18
  38.2 15.1 %collective-permute-start.12 = (bf16[88,1408]{1,0:T(8,128)(2,1)S(1)}, bf16[88,1408]{1,0:T(8,128)(2,1)S(1)}, u32[]{:S(2)}, u32[]{:S(2)}) collective-permute-start(bf16[88,1408]{1,0:T(8,128)(2,1)S(1)} %collective-permute-done.11.refs_4_), channel_id=1, source_target_pairs={{0,2},{2,0},{4,6},{6,4},{8,10},{10,8},{12,14},{14,12},{16,18},{18,... | collective-permute-start | bytes 743432 | tf_op jit(solution)/shard_map/ppermute | solution.py:19
  46.5 8.8 %collective-permute-start.17 = (bf16[88,1408]{1,0:T(8,128)(2,1)S(1)}, bf16[88,1408]{1,0:T(8,128)(2,1)S(1)}, u32[]{:S(2)}, u32[]{:S(2)}) collective-permute-start(bf16[88,1408]{1,0:T(8,128)(2,1)S(1)} %collective-permute-done.16.refs_12_), channel_id=1, source_target_pairs={{0,8},{2,10},{4,12},{6,14},{8,0},{10,2},{12,4},{14,6},{16,24},{18,... | collective-permute-start | bytes 743432 | tf_op jit(solution)/shard_map/ppermute | solution.py:19
  46.5 12.1 %collective-permute-start.19 = (bf16[88,1408]{1,0:T(8,128)(2,1)S(1)}, bf16[88,1408]{1,0:T(8,128)(2,1)S(1)}, u32[]{:S(2)}, u32[]{:S(2)}) collective-permute-start(bf16[88,1408]{1,0:T(8,128)(2,1)S(1)} %collective-permute-done.16.refs_12_), channel_id=1, source_target_pairs={{0,2},{2,0},{4,6},{6,4},{8,10},{10,8},{12,14},{14,12},{16,18},{18,... | collective-permute-start | bytes 743432 | tf_op jit(solution)/shard_map/ppermute | solution.py:19
  49.3 13.7 %collective-permute-start.4 = (bf16[4,64,704]{2,1,0:T(8,128)(2,1)S(1)}, bf16[4,64,704]{2,1,0:T(8,128)(2,1)S(1)}, u32[]{:S(2)}, u32[]{:S(2)}) collective-permute-start(bf16[4,64,704]{2,1,0:T(8,128)(2,1)S(1)} %bitcast.37), channel_id=1, source_target_pairs={{0,4},{2,6},{4,0},{6,2},{8,12},{10,14},{12,8},{14,10},{16,20},{18,... | collective-permute-start | bytes 1081352 | tf_op jit(solution)/shard_map/ppermute | solution.py:18
  53.2 12.1 %collective-permute-start.14 = (bf16[88,1408]{1,0:T(8,128)(2,1)S(1)}, bf16[88,1408]{1,0:T(8,128)(2,1)S(1)}, u32[]{:S(2)}, u32[]{:S(2)}) collective-permute-start(bf16[88,1408]{1,0:T(8,128)(2,1)S(1)} %collective-permute-done.13.refs_6_), channel_id=1, source_target_pairs={{0,2},{2,0},{4,6},{6,4},{8,10},{10,8},{12,14},{14,12},{16,18},{18,... | collective-permute-start | bytes 743432 | tf_op jit(solution)/shard_map/ppermute | solution.py:19
  55.3 10.0 %collective-permute-start.15 = (bf16[88,1408]{1,0:T(8,128)(2,1)S(1)}, bf16[88,1408]{1,0:T(8,128)(2,1)S(1)}, u32[]{:S(2)}, u32[]{:S(2)}) collective-permute-start(bf16[88,1408]{1,0:T(8,128)(2,1)S(1)} %collective-permute-done.8.refs_8_), channel_id=1, source_target_pairs={{0,8},{2,10},{4,12},{6,14},{8,0},{10,2},{12,4},{14,6},{16,24},{18,... | collective-permute-start | bytes 743432 | tf_op jit(solution)/shard_map/ppermute | solution.py:19
  58.6 8.5 %collective-permute-start.18 = (bf16[88,1408]{1,0:T(8,128)(2,1)S(1)}, bf16[88,1408]{1,0:T(8,128)(2,1)S(1)}, u32[]{:S(2)}, u32[]{:S(2)}) collective-permute-start(bf16[88,1408]{1,0:T(8,128)(2,1)S(1)} %collective-permute-done.9.refs_9_), channel_id=1, source_target_pairs={{0,8},{2,10},{4,12},{6,14},{8,0},{10,2},{12,4},{14,6},{16,24},{18,... | collective-permute-start | bytes 743432 | tf_op jit(solution)/shard_map/ppermute | solution.py:19
  58.6 10.2 %collective-permute-start.20 = (bf16[88,1408]{1,0:T(8,128)(2,1)S(1)}, bf16[88,1408]{1,0:T(8,128)(2,1)S(1)}, u32[]{:S(2)}, u32[]{:S(2)}) collective-permute-start(bf16[88,1408]{1,0:T(8,128)(2,1)S(1)} %collective-permute-done.17.refs_14_), channel_id=1, source_target_pairs={{0,2},{2,0},{4,6},{6,4},{8,10},{10,8},{12,14},{14,12},{16,18},{18,... | collective-permute-start | bytes 743432 | tf_op jit(solution)/shard_map/ppermute | solution.py:19
  73.5 2.6 %collective-permute-start.23 = (f32[4,64,704]{2,1,0:T(8,128)S(1)}, f32[4,64,704]{2,1,0:T(8,128)S(1)}, u32[]{:S(2)}, u32[]{:S(2)}) collective-permute-start(f32[4,64,704]{2,1,0:T(8,128)S(1)} %bitcast.49), channel_id=1, source_target_pairs={{0,1},{1,0},{2,3},{3,2},{4,5},{5,4},{6,7},{7,6},{8,9},{9,8},{10,11... | collective-permute-start | bytes 2162696 | tf_op jit(solution)/shard_map/ppermute | solution.py:18
  75.0 2.5 %collective-permute-start.22 = (f32[4,64,704]{2,1,0:T(8,128)S(1)}, f32[4,64,704]{2,1,0:T(8,128)S(1)}, u32[]{:S(2)}, u32[]{:S(2)}) collective-permute-start(f32[4,64,704]{2,1,0:T(8,128)S(1)} %bitcast.50), channel_id=1, source_target_pairs={{0,1},{1,0},{2,3},{3,2},{4,5},{5,4},{6,7},{7,6},{8,9},{9,8},{10,11... | collective-permute-start | bytes 2162696 | tf_op jit(solution)/shard_map/ppermute | solution.py:18
  75.6 12.1 %collective-permute-start.26 = (f32[4,64,704]{2,1,0:T(8,128)S(1)}, f32[4,64,704]{2,1,0:T(8,128)S(1)}, u32[]{:S(2)}, u32[]{:S(2)}) collective-permute-start(f32[4,64,704]{2,1,0:T(8,128)S(1)} %bitcast.48), channel_id=1, source_target_pairs={{0,1},{1,0},{2,3},{3,2},{4,5},{5,4},{6,7},{7,6},{8,9},{9,8},{10,11... | collective-permute-start | bytes 2162696 | tf_op jit(solution)/shard_map/ppermute | solution.py:18
  75.7 23.0 %collective-permute-start.21 = (f32[4,64,704]{2,1,0:T(8,128)S(1)}, f32[4,64,704]{2,1,0:T(8,128)S(1)}, u32[]{:S(2)}, u32[]{:S(2)}) collective-permute-start(f32[4,64,704]{2,1,0:T(8,128)S(1)} %bitcast.47), channel_id=1, source_target_pairs={{0,1},{1,0},{2,3},{3,2},{4,5},{5,4},{6,7},{7,6},{8,9},{9,8},{10,11... | collective-permute-start | bytes 2162696 | tf_op jit(solution)/shard_map/ppermute | solution.py:18
  76.2 11.2 %collective-permute-start.24 = (bf16[4,64,704]{2,1,0:T(8,128)(2,1)S(1)}, bf16[4,64,704]{2,1,0:T(8,128)(2,1)S(1)}, u32[]{:S(2)}, u32[]{:S(2)}) collective-permute-start(bf16[4,64,704]{2,1,0:T(8,128)(2,1)S(1)} %bitcast.42), channel_id=1, source_target_pairs={{0,4},{2,6},{4,0},{6,2},{8,12},{10,14},{12,8},{14,10},{16,20},{18,... | collective-permute-start | bytes 1081352 | tf_op jit(solution)/shard_map/ppermute | solution.py:18
  87.4 16.3 %collective-permute-start.25 = (bf16[4,64,704]{2,1,0:T(8,128)(2,1)S(1)}, bf16[4,64,704]{2,1,0:T(8,128)(2,1)S(1)}, u32[]{:S(2)}, u32[]{:S(2)}) collective-permute-start(bf16[4,64,704]{2,1,0:T(8,128)(2,1)S(1)} %bitcast.40), channel_id=1, source_target_pairs={{0,4},{2,6},{4,0},{6,2},{8,12},{10,14},{12,8},{14,10},{16,20},{18,... | collective-permute-start | bytes 1081352 | tf_op jit(solution)/shard_map/ppermute | solution.py:18
  88.1 1.4 %collective-permute-start.27 = (f32[256,2]{1,0:T(8,128)S(1)}, f32[256,2]{1,0:T(8,128)S(1)}, u32[]{:S(2)}, u32[]{:S(2)}) collective-permute-start(f32[256,2]{1,0:T(8,128)S(1)} %get-tuple-element.77.mine), channel_id=1, source_target_pairs={{0,1},{1,0},{2,3},{3,2},{4,5},{5,4},{6,7},{7,6},{8,9},{9,8},{10,11... | collective-permute-start | bytes 6152 | tf_op jit(solution)/shard_map/ppermute | solution.py:19
  90.4 20.5 %collective-permute-start.35 = (bf16[3,64,704]{2,1,0:T(8,128)(2,1)S(1)}, bf16[3,64,704]{2,1,0:T(8,128)(2,1)S(1)}, u32[]{:S(2)}, u32[]{:S(2)}) collective-permute-start(bf16[3,64,704]{2,1,0:T(8,128)(2,1)S(1)} %get-tuple-element.88), channel_id=1, source_target_pairs={{0,2},{2,0},{4,6},{6,4},{8,10},{10,8},{12,14},{14,12},{16,18},{18,... | collective-permute-start | bytes 811016 | tf_op jit(solution)/shard_map/ppermute | solution.py:19
  96.7 4.4 %collective-permute-start.28 = (f32[2,8,704]{2,1,0:T(8,128)S(1)}, f32[2,8,704]{2,1,0:T(8,128)S(1)}, u32[]{:S(2)}, u32[]{:S(2)}) collective-permute-start(f32[2,8,704]{2,1,0:T(8,128)S(1)} %get-tuple-element.81), channel_id=1, source_target_pairs={{0,2},{2,0},{4,6},{6,4},{8,10},{10,8},{12,14},{14,12},{16,18},{18,... | collective-permute-start | bytes 135176 | tf_op jit(solution)/shard_map/ppermute | solution.py:19
  97.0 4.1 %collective-permute-start.29 = (f32[2,8,704]{2,1,0:T(8,128)S(1)}, f32[2,8,704]{2,1,0:T(8,128)S(1)}, u32[]{:S(2)}, u32[]{:S(2)}) collective-permute-start(f32[2,8,704]{2,1,0:T(8,128)S(1)} %get-tuple-element.82), channel_id=1, source_target_pairs={{0,4},{2,6},{4,0},{6,2},{8,12},{10,14},{12,8},{14,10},{16,20},{18,... | collective-permute-start | bytes 135176 | tf_op jit(solution)/shard_map/ppermute | solution.py:19
  98.7 5.0 %collective-permute-start.30 = (f32[2,8,704]{2,1,0:T(8,128)S(1)}, f32[2,8,704]{2,1,0:T(8,128)S(1)}, u32[]{:S(2)}, u32[]{:S(2)}) collective-permute-start(f32[2,8,704]{2,1,0:T(8,128)S(1)} %get-tuple-element.83), channel_id=1, source_target_pairs={{0,6},{2,4},{4,2},{6,0},{8,14},{10,12},{12,10},{14,8},{16,22},{18,... | collective-permute-start | bytes 135176 | tf_op jit(solution)/shard_map/ppermute | solution.py:19
  104.7 8.4 %collective-permute-start.34 = (f32[2,8,704]{2,1,0:T(8,128)S(1)}, f32[2,8,704]{2,1,0:T(8,128)S(1)}, u32[]{:S(2)}, u32[]{:S(2)}) collective-permute-start(f32[2,8,704]{2,1,0:T(8,128)S(1)} %get-tuple-element.86), channel_id=1, source_target_pairs={{0,8},{2,10},{4,12},{6,14},{8,0},{10,2},{12,4},{14,6},{16,24},{18,... | collective-permute-start | bytes 135176 | tf_op jit(solution)/shard_map/ppermute | solution.py:19
  105.0 8.2 %collective-permute-start.33 = (f32[2,8,704]{2,1,0:T(8,128)S(1)}, f32[2,8,704]{2,1,0:T(8,128)S(1)}, u32[]{:S(2)}, u32[]{:S(2)}) collective-permute-start(f32[2,8,704]{2,1,0:T(8,128)S(1)} %get-tuple-element.86), channel_id=1, source_target_pairs={{0,16},{2,18},{4,20},{6,22},{8,24},{10,26},{12,28},{14,30},{16,0},... | collective-permute-start | bytes 135176 | tf_op jit(solution)/shard_map/ppermute | solution.py:19
  106.8 6.4 %collective-permute-start.32 = (f32[2,8,704]{2,1,0:T(8,128)S(1)}, f32[2,8,704]{2,1,0:T(8,128)S(1)}, u32[]{:S(2)}, u32[]{:S(2)}) collective-permute-start(f32[2,8,704]{2,1,0:T(8,128)S(1)} %get-tuple-element.86), channel_id=1, source_target_pairs={{0,24},{2,26},{4,28},{6,30},{8,16},{10,18},{12,20},{14,22},{16,8},... | collective-permute-start | bytes 135176 | tf_op jit(solution)/shard_map/ppermute | solution.py:19
  109.1 7.8 %collective-permute-start.31 = (bf16[3,64,704]{2,1,0:T(8,128)(2,1)S(1)}, bf16[3,64,704]{2,1,0:T(8,128)(2,1)S(1)}, u32[]{:S(2)}, u32[]{:S(2)}) collective-permute-start(bf16[3,64,704]{2,1,0:T(8,128)(2,1)S(1)} %get-tuple-element.85), channel_id=1, source_target_pairs={{0,2},{2,0},{4,6},{6,4},{8,10},{10,8},{12,14},{14,12},{16,18},{18,... | collective-permute-start | bytes 811016 | tf_op jit(solution)/shard_map/ppermute | solution.py:19
  110.9 7.5 %collective-permute-start.36 = (bf16[3,64,704]{2,1,0:T(8,128)(2,1)S(1)}, bf16[3,64,704]{2,1,0:T(8,128)(2,1)S(1)}, u32[]{:S(2)}, u32[]{:S(2)}) collective-permute-start(bf16[3,64,704]{2,1,0:T(8,128)(2,1)S(1)} %collective-permute-done.35), channel_id=1, source_target_pairs={{0,4},{4,8},{8,12},{12,16},{16,20},{20,24},{24,28},{6,2},{10,6},{1... | collective-permute-start | bytes 811016 | tf_op jit(solution)/shard_map/ppermute | solution.py:49
  113.2 9.3 %collective-permute-start.39 = (f32[2,8,704]{2,1,0:T(8,128)S(1)}, f32[2,8,704]{2,1,0:T(8,128)S(1)}, u32[]{:S(2)}, u32[]{:S(2)}) collective-permute-start(f32[2,8,704]{2,1,0:T(8,128)S(1)} %add_add_fusion.c0), channel_id=1, source_target_pairs={{0,6},{2,4},{4,2},{6,0},{8,14},{10,12},{12,10},{14,8},{16,22},{18,... | collective-permute-start | bytes 135176 | tf_op jit(solution)/shard_map/ppermute | solution.py:19
  114.6 7.8 %collective-permute-start.38 = (f32[2,8,704]{2,1,0:T(8,128)S(1)}, f32[2,8,704]{2,1,0:T(8,128)S(1)}, u32[]{:S(2)}, u32[]{:S(2)}) collective-permute-start(f32[2,8,704]{2,1,0:T(8,128)S(1)} %add_add_fusion.c0), channel_id=1, source_target_pairs={{0,4},{2,6},{4,0},{6,2},{8,12},{10,14},{12,8},{14,10},{16,20},{18,... | collective-permute-start | bytes 135176 | tf_op jit(solution)/shard_map/ppermute | solution.py:19
  115.8 6.7 %collective-permute-start.37 = (f32[2,8,704]{2,1,0:T(8,128)S(1)}, f32[2,8,704]{2,1,0:T(8,128)S(1)}, u32[]{:S(2)}, u32[]{:S(2)}) collective-permute-start(f32[2,8,704]{2,1,0:T(8,128)S(1)} %add_add_fusion.c0), channel_id=1, source_target_pairs={{0,2},{2,0},{4,6},{6,4},{8,10},{10,8},{12,14},{14,12},{16,18},{18,... | collective-permute-start | bytes 135176 | tf_op jit(solution)/shard_map/ppermute | solution.py:19
